TPU v7x, 256 devices: a whole 4x4x8 slice. The times are simulated.
256 devices in a mesh: span: 64 (over x, z, core), head: 4 (over y).
Axes of the slice: x: 4, y: 4, z: 8, core: 2. Of those that a mesh axis runs over, the one named last changes fastest.
Arguments:
- query: bfloat16 [131072, 2048], P('span', 'head'), may hold values from -27 to 27
- keys: bfloat16 [128, 128, 2048], P('span', 'head'), may hold values from -11 to 11
- values: bfloat16 [128, 128, 2048], P('span', 'head'), may hold values from -6 to 6
- grad_out: bfloat16 [131072, 2048], P('span', 'head'), may hold values from -6 to 6
- neighbour: int32 [2048], replicated, may hold values from 0 to 127, as said below
Outputs:
- attended: bfloat16 [131072, 2048], P('span', 'head')
- grad_query: bfloat16 [131072, 2048], P('span', 'head')
- grad_keys: bfloat16 [128, 128, 2048], P('span', 'head')
- grad_values: bfloat16 [128, 128, 2048], P('span', 'head')
Inputs may be any that keep to these rules, and one draw needn't show every extreme that they name: Neighbour m is owned by index m // 2 of span, the block of keys and values that holds it. Among the 32 spans of one index of span at most one names a neighbour of any given owner, and some owner is named by exactly one span of every index of span.
All inputs are finite; a program needn't handle non-finite values.
Results may differ from a plain program's by a relative error of at most 0.03.
Values may be sent and summed in bfloat16 or wider, within the bound.
No kernel may reach another device: no remote copies, remote signals or barrier semaphores. Data moves between devices by JAX's collectives and lax.ppermute only.
A program may use at most 128 MiB of HBM per device.

v0:
```python
import math

import jax
import jax.numpy as jnp
from jax import lax
from jax.experimental import pallas as pl
from jax.experimental.pallas import tpu as pltpu
from jax.sharding import Mesh, PartitionSpec as P

HS = 128
SPAN = 64
NBLEN = 128
X, Y, Z, C = 4, 4, 8, 2
NB = 2
GROUP = X * NB
HALF = Z * GROUP
SLOTS = C * HALF
HEADS = X * Y
PIECE = NBLEN // Y
SCALE = 1.0 / math.sqrt(HS)
SCALE_LOG2 = SCALE * math.log2(math.e)
BF = jnp.bfloat16
F32 = jnp.float32
EARLY, LATE = (0, 7, 1, 6, 2), (5, 3, 4)
ORDER = EARLY + LATE
N_EARLY, N_LATE = len(EARLY) * GROUP, len(LATE) * GROUP
BATCH = 16
MIB = 1024 * 1024


def shift(a, axis, size, by):
    return lax.ppermute(a, axis, [(i, (i + by) % size) for i in range(size)])


def ring_gather(block):
    half = GROUP // 2
    right1, left1 = shift(block, "z", Z, 1), shift(block, "z", Z, -1)
    right2, left2 = shift(right1, "z", Z, 1), shift(left1, "z", Z, -1)
    early = jnp.concatenate([block, right1, left1, right2, left2])
    right3, left3 = shift(right2, "z", Z, 1), shift(left2, "z", Z, -1)
    far = [shift(right3[:half], "z", Z, 1), shift(left3[half:], "z", Z, -1)]
    late = jnp.concatenate([right3, left3] + far)
    return early, late


def ring_reduce(blocks):
    half = GROUP // 2
    far = blocks[Z // 2]
    right = shift(far[:half], "z", Z, 1)
    left = shift(far[half:], "z", Z, -1)
    right = jnp.concatenate([right + blocks[3][:half], blocks[3][half:]])
    left = jnp.concatenate([blocks[Z - 3][:half], left + blocks[Z - 3][half:]])
    for k in (2, 1):
        right = shift(right, "z", Z, 1) + blocks[k]
        left = shift(left, "z", Z, -1) + blocks[Z - k]
    return shift(right, "z", Z, 1), shift(left, "z", Z, -1)


def dot(a, b, ca, cb):
    return lax.dot_general(a, b, (((ca,), (cb,)), ((), ())), preferred_element_type=F32)


def attention_kernel(ids, tokens, *refs):
    keys, values = refs[:4], refs[4:8]
    reply, dk_outs, dv_outs = refs[8], refs[9:12], refs[12:15]
    tbuf, kbuf, vbuf, obuf, dk, dv, low, t_sems, kv_sems, o_sems, s_sems = refs[15:]
    loads = []
    for sources, buf in ((keys, kbuf), (values, vbuf)):
        at = 0
        for source in sources:
            rows = source.shape[0]
            loads.append(
                pltpu.make_async_copy(source, buf.at[pl.ds(at, rows)], kv_sems.at[len(loads)])
            )
            at += rows

    def token_load(part):
        return pltpu.make_async_copy(tokens.at[part], tbuf.at[part], t_sems.at[part])

    def token_store(part):
        return pltpu.make_async_copy(obuf.at[part], reply.at[part], o_sems.at[part])

    for load in loads:
        load.start()
    for part in range(X):
        token_load(part).start()

    def clear(i, _):
        dk[i] = jnp.zeros((NBLEN, HS), F32)
        dv[i] = jnp.zeros((NBLEN, HS), F32)
        return 0

    lax.fori_loop(0, SLOTS, clear, 0, unroll=2)
    for load in loads:
        load.wait()
    steps_per_part = tokens.shape[2] // (BATCH * SPAN)

    def body(step, _):
        part, inner = step // steps_per_part, step % steps_per_part

        @pl.when(inner == 0)
        def _():
            token_load(part).wait()

        q_ref, g_ref = tbuf.at[part, 0], tbuf.at[part, 1]
        att_ref, gq_ref = obuf.at[part, 0], obuf.at[part, 1]
        rows = [
            pl.ds(pl.multiple_of((inner * BATCH + i) * SPAN, SPAN), SPAN) for i in range(BATCH)
        ]
        named = [ids[step * BATCH + i] for i in range(BATCH)]
        qs = [q_ref[r, :] for r in rows]
        gs = [g_ref[r, :] for r in rows]
        scores = [dot(q, kbuf[n], 1, 1) * SCALE_LOG2 for q, n in zip(qs, named)]
        dprobs = [dot(g, vbuf[n], 1, 1) for g, n in zip(gs, named)]
        expo = [jnp.exp2(s - jnp.max(s, axis=-1, keepdims=True)) for s in scores]
        probs = [e * (1.0 / jnp.sum(e, axis=-1, keepdims=True)) for e in expo]
        probs_low = [p.astype(BF) for p in probs]
        att = [dot(p, vbuf[n], 1, 0).astype(BF) for p, n in zip(probs_low, named)]
        for r, a in zip(rows, att):
            att_ref[r, :] = a
        delta = [
            jnp.sum(g.astype(F32) * a.astype(F32), axis=-1, keepdims=True) for g, a in zip(gs, att)
        ]
        ds = [(p * (d - t)).astype(BF) for p, d, t in zip(probs, dprobs, delta)]
        for r, d, n in zip(rows, ds, named):
            gq_ref[r, :] = (dot(d, kbuf[n], 1, 0) * SCALE).astype(BF)
        value_terms = [dot(p, g, 0, 0) for p, g in zip(probs_low, gs)]
        key_terms = [dot(d, q, 0, 0) for d, q in zip(ds, qs)]
        for n, vt, kt in zip(named, value_terms, key_terms):
            dv[n] += vt
            dk[n] += kt

        @pl.when(inner == steps_per_part - 1)
        def _():
            token_store(part).start()

        return 0

    lax.fori_loop(0, X * steps_per_part, body, 0)

    stores = []
    spans = ((HALF + N_EARLY, SLOTS), (HALF, HALF + N_EARLY), (0, HALF))
    for piece, (first, last) in enumerate(spans):
        for which, (sums, outs) in enumerate(((dk, dk_outs), (dv, dv_outs))):

            def finish(i, _):
                value = sums[i]
                low[which, i] = (value * SCALE if which == 0 else value).astype(BF)
                return 0

            lax.fori_loop(first, last, finish, 0, unroll=2)
            store = pltpu.make_async_copy(
                low.at[which, pl.ds(first, last - first)], outs[piece], s_sems.at[2 * piece + which]
            )
            store.start()
            stores.append(store)
    for store in stores:
        store.wait()
    for part in range(X):
        token_store(part).wait()


def attention(ids, tokens, parts):
    hbm = pl.BlockSpec(memory_space=pl.ANY)
    sums = [
        jax.ShapeDtypeStruct((n, NBLEN, HS), BF) for n in (N_LATE, N_EARLY, HALF)
    ]
    low = pltpu.VMEM((SLOTS, NBLEN, HS), BF)
    wide = pltpu.VMEM((SLOTS, NBLEN, HS), F32)
    dma = pltpu.SemaphoreType.DMA
    return pl.pallas_call(
        attention_kernel,
        grid_spec=pltpu.PrefetchScalarGridSpec(
            num_scalar_prefetch=1,
            grid=(1,),
            in_specs=[hbm] * 9,
            out_specs=[hbm] * 7,
            scratch_shapes=[
                pltpu.VMEM(tokens.shape, BF),
                low,
                low,
                pltpu.VMEM(tokens.shape, BF),
                wide,
                wide,
                pltpu.VMEM((2, SLOTS, NBLEN, HS), BF),
                dma((X,)),
                dma((8,)),
                dma((X,)),
                dma((6,)),
            ],
        ),
        out_shape=[jax.ShapeDtypeStruct(tokens.shape, BF)] + sums + sums,
        compiler_params=pltpu.CompilerParams(vmem_limit_bytes=56 * MIB),
        name="attention",
    )(ids, tokens, *parts)


def split_heads(a, b):
    tokens = a.shape[0]
    rows = 512

    def kernel(a_ref, b_ref, out):
        for h in range(X):
            at = pl.ds(h * HS, HS)
            out[h, 0] = a_ref[:, at]
            out[h, 1] = b_ref[:, at]

    wide = pl.BlockSpec((rows, X * HS), lambda i: (i, 0))
    return pl.pallas_call(
        kernel,
        grid=(tokens // rows,),
        in_specs=[wide, wide],
        out_specs=pl.BlockSpec((X, 2, rows, HS), lambda i: (0, 0, i, 0)),
        out_shape=jax.ShapeDtypeStruct((X, 2, tokens, HS), BF),
        name="split_heads",
    )(a, b)


def join_heads(a):
    tokens = a.shape[2]
    rows = 512

    def kernel(a_ref, out0, out1):
        for h in range(X):
            at = pl.ds(h * HS, HS)
            out0[:, at] = a_ref[h, 0]
            out1[:, at] = a_ref[h, 1]

    wide = pl.BlockSpec((rows, X * HS), lambda i: (i, 0))
    return pl.pallas_call(
        kernel,
        grid=(tokens // rows,),
        in_specs=[pl.BlockSpec((X, 2, rows, HS), lambda i: (0, 0, i, 0))],
        out_specs=[wide, wide],
        out_shape=[jax.ShapeDtypeStruct((tokens, X * HS), BF)] * 2,
        name="join_heads",
    )(a)


def pack_encodings(keys, values):
    def kernel(k_ref, v_ref, out):
        for h in range(HEADS):
            at = pl.ds(h * HS, HS)
            out[h, 0] = k_ref[:, :, at]
            out[h, 1] = v_ref[:, :, at]

    return pl.pallas_call(
        kernel,
        out_shape=jax.ShapeDtypeStruct((HEADS, 2, NB, PIECE, HS), BF),
        name="pack_encodings",
    )(keys, values)


def unpack_encodings(a):
    def kernel(a_ref, k_ref, v_ref):
        for h in range(HEADS):
            at = pl.ds(h * HS, HS)
            k_ref[:, :, at] = a_ref[h, 0]
            v_ref[:, :, at] = a_ref[h, 1]

    return pl.pallas_call(
        kernel,
        out_shape=[jax.ShapeDtypeStruct((NB, PIECE, HEADS * HS), BF)] * 2,
        name="unpack_encodings",
    )(a)


def final_sums(key_terms, value_terms):
    def kernel(*refs):
        out = refs[-1]
        for which in range(2):
            terms = refs[4 * which : 4 * which + 4]
            for x in range(X):
                for n in range(NB):
                    total = sum(t[x * NB + n].astype(F32) for t in terms).astype(BF)
                    for y in range(Y):
                        out[y, x, which, n] = total[y * PIECE : (y + 1) * PIECE]

    block = pl.BlockSpec((GROUP, NBLEN, HS), lambda i: (0, 0, 0))
    shape = (Y, X, 2, NB, PIECE, HS)
    return pl.pallas_call(
        kernel,
        grid=(1,),
        in_specs=[block] * 8,
        out_specs=pl.BlockSpec(shape, lambda i: (0,) * 6),
        out_shape=jax.ShapeDtypeStruct(shape, BF),
        name="final_sums",
    )(*key_terms, *value_terms)


def per_device(query, keys, values, grad_out, neighbour):
    z_self, c_self = lax.axis_index("z"), lax.axis_index("core")

    both = pack_encodings(keys, values)
    both = lax.all_to_all(both, ("head", "x"), split_axis=0, concat_axis=0, tiled=True)
    both = both.reshape(Y, X, 2, NB, PIECE, HS)
    both = jnp.transpose(both, (2, 1, 3, 0, 4, 5)).reshape(2, GROUP, NBLEN, HS)

    tokens = split_heads(query, grad_out)
    tokens = lax.all_to_all(tokens, "x", split_axis=0, concat_axis=0, tiled=True)

    parts = []
    for block in (both[0], both[1]):
        early, late = ring_gather(block)
        parts += [early, late, shift(early, "core", C, 1), shift(late, "core", C, 1)]

    table = neighbour.reshape(X, Z, C, -1)
    table = lax.dynamic_index_in_dim(table, z_self, 1, keepdims=False)
    table = lax.dynamic_index_in_dim(table, c_self, 1, keepdims=False).reshape(-1)
    owner, local = table // NB, table % NB
    owner_x, owner_z, owner_c = owner // (Z * C), (owner // C) % Z, owner % C
    other = (owner_c != c_self).astype(jnp.int32)
    offset = (owner_z - z_self) % Z
    place = sum(jnp.where(offset == o, i, 0) for i, o in enumerate(ORDER))
    ids = ((other * Z + place) * X + owner_x) * NB + local

    reply, *sums = attention(ids, tokens, parts)
    reply = lax.all_to_all(reply, "x", split_axis=0, concat_axis=0, tiled=True)

    terms = []
    for late, early, own in (sums[:3], sums[3:]):
        got_late, got_early = shift(late, "core", C, 1), shift(early, "core", C, 1)

        def block(k):
            place = ORDER.index(k)
            at = place * GROUP
            got = got_early[at : at + GROUP] if place < len(EARLY) else got_late[at - N_EARLY : at - N_EARLY + GROUP]
            return own[at : at + GROUP] + got

        right, left = ring_reduce([None] + [block(k) for k in range(1, Z)])
        terms.append((own, got_early, right, left))

    grads = final_sums(*terms).reshape(HEADS, 2, NB, PIECE, HS)
    grads, reply = lax.optimization_barrier((grads, reply))
    grads = lax.all_to_all(grads, ("head", "x"), split_axis=0, concat_axis=0, tiled=True)
    attended, grad_query = join_heads(reply)
    grad_keys, grad_values = unpack_encodings(grads)
    return attended, grad_query, grad_keys, grad_values


def solution(mesh):
    fine = Mesh(mesh.devices.reshape(X, Z, C, Y), ("x", "z", "core", "head"))
    span = ("x", "z", "core")
    tokens, encodings = P(span, "head"), P(span, "head", None)
    return jax.shard_map(
        per_device,
        mesh=fine,
        in_specs=(tokens, encodings, encodings, tokens, P()),
        out_specs=(tokens, tokens, encodings, encodings),
        check_vma=False,
    )
```

profile of v0, /device:TPU:1, one launch (start us, length us, event | category | flops | bytes accessed | tf_op | source)
XLA Modules:
  0.0 178.7 jit_solution(3216699884042132706)
XLA Ops:
  2.5 7.6 %all-to-all-start.1 = ((bf16[16,2,2,32,128]{4,3,2,1,0:T(8,128)(2,1)}), bf16[16,2,2,32,128]{4,3,2,1,0:T(8,128)(2,1)S(1)}, u32[]{:S(2)}, u32[]{:S(2)}) async-start(bf16[16,2,2,32,128]{4,3,2,1,0:T(8,128)(2,1)} %pack_encodings.1), calls=%async_computation.1 | async-start | bytes 1048576 | tf_op jit(solution)/shard_map/all_to_all | solution.py:295
  10.1 4.9 %split_heads.1 = bf16[4,2,2048,128]{3,2,1,0:T(8,128)(2,1)} custom-call(bf16[2048,512]{1,0:T(8,128)(2,1)} %a_ref.1, bf16[2048,512]{1,0:T(8,128)(2,1)} %b_ref.1), custom_call_target="tpu_custom_call" | custom-call | tf_op jit(solution)/shard_map/split_heads/pallas_call | solution.py:209
  15.1 5.6 %all-to-all-done.1 = bf16[16,2,2,32,128]{4,3,2,1,0:T(8,128)(2,1)S(1)} async-done(((bf16[16,2,2,32,128]{4,3,2,1,0:T(8,128)(2,1)}), bf16[16,2,2,32,128]{4,3,2,1,0:T(8,128)(2,1)S(1)}, u32[]{:S(2)}, u32[]{:S(2)}) %all-to-all-start.1) | async-done | bytes 524320 | tf_op jit(solution)/shard_map/all_to_all | solution.py:295
  20.6 4.9 %all-to-all-start = ((bf16[4,2,2048,128]{3,2,1,0:T(8,128)(2,1)}), bf16[4,2,2048,128]{3,2,1,0:T(8,128)(2,1)}, u32[]{:S(2)}, u32[]{:S(2)}) async-start(bf16[4,2,2048,128]{3,2,1,0:T(8,128)(2,1)} %split_heads.1), calls=%async_computation | async-start | bytes 8388608 | tf_op jit(solution)/shard_map/all_to_all | solution.py:300
  25.6 5.7 %collective-permute-start.1 = (bf16[8,128,128]{2,1,0:T(8,128)(2,1)S(1)}, bf16[8,128,128]{2,1,0:T(8,128)(2,1)S(1)}, u32[]{:S(2)}, u32[]{:S(2)}) collective-permute-start(bf16[8,128,128]{2,1,0:T(8,128)(2,1)S(1)} %bitcast.13), channel_id=1, source_target_pairs={{0,56},{8,0},{16,8},{24,16},{32,24},{40,32},{48,40},{56,48},{1,57}... | collective-permute-start | bytes 786440 | tf_op jit(solution)/shard_map/ppermute | solution.py:32
  34.9 3.5 %collective-permute-start.3 = (bf16[8,128,128]{2,1,0:T(8,128)(2,1)S(1)}, bf16[8,128,128]{2,1,0:T(8,128)(2,1)S(1)}, u32[]{:S(2)}, u32[]{:S(2)}) collective-permute-start(bf16[8,128,128]{2,1,0:T(8,128)(2,1)S(1)} %collective-permute-done.1), channel_id=1, source_target_pairs={{0,56},{8,0},{16,8},{24,16},{32,24},{40,32},{48,40},{56,48},{1,57}... | collective-permute-start | bytes 786440 | tf_op jit(solution)/shard_map/ppermute | solution.py:32
  40.5 3.5 %collective-permute-start.13 = (bf16[8,128,128]{2,1,0:T(8,128)(2,1)S(1)}, bf16[8,128,128]{2,1,0:T(8,128)(2,1)S(1)}, u32[]{:S(2)}, u32[]{:S(2)}) collective-permute-start(bf16[8,128,128]{2,1,0:T(8,128)(2,1)S(1)} %collective-permute-done.11), channel_id=1, source_target_pairs={{0,56},{8,0},{16,8},{24,16},{32,24},{40,32},{48,40},{56,48},{1,57}... | collective-permute-start | bytes 786440 | tf_op jit(solution)/shard_map/ppermute | solution.py:32
  46.1 3.5 %collective-permute-start.5 = (bf16[8,128,128]{2,1,0:T(8,128)(2,1)S(1)}, bf16[8,128,128]{2,1,0:T(8,128)(2,1)S(1)}, u32[]{:S(2)}, u32[]{:S(2)}) collective-permute-start(bf16[8,128,128]{2,1,0:T(8,128)(2,1)S(1)} %collective-permute-done.3), channel_id=1, source_target_pairs={{0,56},{8,0},{16,8},{24,16},{32,24},{40,32},{48,40},{56,48},{1,57}... | collective-permute-start | bytes 786440 | tf_op jit(solution)/shard_map/ppermute | solution.py:32
  51.8 3.5 %collective-permute-start.15 = (bf16[8,128,128]{2,1,0:T(8,128)(2,1)S(1)}, bf16[8,128,128]{2,1,0:T(8,128)(2,1)S(1)}, u32[]{:S(2)}, u32[]{:S(2)}) collective-permute-start(bf16[8,128,128]{2,1,0:T(8,128)(2,1)S(1)} %collective-permute-done.13), channel_id=1, source_target_pairs={{0,56},{8,0},{16,8},{24,16},{32,24},{40,32},{48,40},{56,48},{1,57}... | collective-permute-start | bytes 786440 | tf_op jit(solution)/shard_map/ppermute | solution.py:32
  55.4 5.7 %collective-permute-start.18 = (bf16[40,128,128]{2,1,0:T(8,128)(2,1)S(1)}, bf16[40,128,128]{2,1,0:T(8,128)(2,1)}, u32[]{:S(2)}, u32[]{:S(2)}) collective-permute-start(bf16[40,128,128]{2,1,0:T(8,128)(2,1)S(1)} %constant_dynamic-update-slice_fusion.9.refs_4_), channel_id=1, source_target_pairs={{0,4},{4,0},{1,5},{5,1},{2,6},{6,2},{3,7},{7,3},{8,12},{12,8},{9,1... | collective-permute-start | bytes 3932168 | tf_op jit(solution)/shard_map/ppermute | solution.py:32
  62.8 3.7 %collective-permute-start.7 = (bf16[4,128,128]{2,1,0:T(8,128)(2,1)S(1)}, bf16[4,128,128]{2,1,0:T(8,128)(2,1)S(1)}, u32[]{:S(2)}, u32[]{:S(2)}) collective-permute-start(bf16[4,128,128]{2,1,0:T(8,128)(2,1)S(1)} %slice.188), channel_id=1, source_target_pairs={{0,56},{8,0},{16,8},{24,16},{32,24},{40,32},{48,40},{56,48},{1,57}... | collective-permute-start | bytes 393224 | tf_op jit(solution)/shard_map/ppermute | solution.py:32
  66.6 3.6 %collective-permute-done.14 = bf16[8,128,128]{2,1,0:T(8,128)(2,1)S(1)} collective-permute-done((bf16[8,128,128]{2,1,0:T(8,128)(2,1)S(1)}, bf16[8,128,128]{2,1,0:T(8,128)(2,1)S(1)}, u32[]{:S(2)}, u32[]{:S(2)}) %collective-permute-start.14) | collective-permute-done | bytes 262176 | tf_op jit(solution)/shard_map/ppermute | solution.py:32
  83.6 20.7 %attention.1 = (bf16[4,2,2048,128]{3,2,1,0:T(8,128)(2,1)}, bf16[24,128,128]{2,1,0:T(8,128)(2,1)}, bf16[40,128,128]{2,1,0:T(8,128)(2,1)}, bf16[64,128,128]{2,1,0:...) custom-call(s32[128]{0:T(128)} %fusion.8.ids, ...), custom_call_target="tpu_custom_call" | custom-call | tf_op jit(solution)/shard_map/attention/pallas_call | solution.py:171
  104.9 5.0 %all-to-all-start.2 = ((bf16[4,2,2048,128]{3,2,1,0:T(8,128)(2,1)}), bf16[4,2,2048,128]{3,2,1,0:T(8,128)(2,1)}, u32[]{:S(2)}, u32[]{:S(2)}) async-start(bf16[4,2,2048,128]{3,2,1,0:T(8,128)(2,1)} %get-tuple-element.23), calls=%async_computation.2 | async-start | bytes 8388608 | tf_op jit(solution)/shard_map/all_to_all | solution.py:318
  118.5 5.1 %collective-permute-done.32 = bf16[4,128,128]{2,1,0:T(8,128)(2,1)S(1)} collective-permute-done((bf16[4,128,128]{2,1,0:T(8,128)(2,1)S(1)}, bf16[4,128,128]{2,1,0:T(8,128)(2,1)S(1)}, u32[]{:S(2)}, u32[]{:S(2)}) %collective-permute-start.32) | collective-permute-done | bytes 131104 | tf_op jit(solution)/shard_map/ppermute | solution.py:32
  125.2 3.7 %collective-permute-done.23 = bf16[8,128,128]{2,1,0:T(8,128)(2,1)S(1)} collective-permute-done((bf16[8,128,128]{2,1,0:T(8,128)(2,1)S(1)}, bf16[8,128,128]{2,1,0:T(8,128)(2,1)S(1)}, u32[]{:S(2)}, u32[]{:S(2)}) %collective-permute-start.23) | collective-permute-done | bytes 262176 | tf_op jit(solution)/shard_map/ppermute | solution.py:32
  130.8 3.8 %collective-permute-done.33 = bf16[8,128,128]{2,1,0:T(8,128)(2,1)S(1)} collective-permute-done((bf16[8,128,128]{2,1,0:T(8,128)(2,1)S(1)}, bf16[8,128,128]{2,1,0:T(8,128)(2,1)S(1)}, u32[]{:S(2)}, u32[]{:S(2)}) %collective-permute-start.33) | collective-permute-done | bytes 262176 | tf_op jit(solution)/shard_map/ppermute | solution.py:32
  137.4 3.9 %collective-permute-done.28 = bf16[8,128,128]{2,1,0:T(8,128)(2,1)S(1)} collective-permute-done((bf16[8,128,128]{2,1,0:T(8,128)(2,1)S(1)}, bf16[8,128,128]{2,1,0:T(8,128)(2,1)S(1)}, u32[]{:S(2)}, u32[]{:S(2)}) %collective-permute-start.28) | collective-permute-done | bytes 262176 | tf_op jit(solution)/shard_map/ppermute | solution.py:32
  142.9 4.0 %collective-permute-done.38 = bf16[8,128,128]{2,1,0:T(8,128)(2,1)S(1)} collective-permute-done((bf16[8,128,128]{2,1,0:T(8,128)(2,1)S(1)}, bf16[8,128,128]{2,1,0:T(8,128)(2,1)S(1)}, u32[]{:S(2)}, u32[]{:S(2)}) %collective-permute-start.38) | collective-permute-done | bytes 262176 | tf_op jit(solution)/shard_map/ppermute | solution.py:32
  148.5 4.0 %collective-permute-done.29.refs_3_ = bf16[8,128,128]{2,1,0:T(8,128)(2,1)S(1)} collective-permute-done((bf16[8,128,128]{2,1,0:T(8,128)(2,1)S(1)}, bf16[8,128,128]{2,1,0:T(8,128)(2,1)S(1)}, u32[]{:S(2)}, u32[]{:S(2)}) %collective-permute-start.29) | collective-permute-done | bytes 262176 | tf_op jit(solution)/shard_map/ppermute | solution.py:32
  152.5 5.6 %collective-permute-done.39.refs_7_ = bf16[8,128,128]{2,1,0:T(8,128)(2,1)S(1)} collective-permute-done((bf16[8,128,128]{2,1,0:T(8,128)(2,1)S(1)}, bf16[8,128,128]{2,1,0:T(8,128)(2,1)S(1)}, u32[]{:S(2)}, u32[]{:S(2)}) %collective-permute-start.39) | collective-permute-done | bytes 262176 | tf_op jit(solution)/shard_map/ppermute | solution.py:32
  162.1 4.7 %all-to-all-start.3 = ((bf16[16,2,2,32,128]{4,3,2,1,0:T(8,128)(2,1)}), bf16[16,2,2,32,128]{4,3,2,1,0:T(8,128)(2,1)S(1)}, u32[]{:S(2)}, u32[]{:S(2)}) async-start(bf16[16,2,2,32,128]{4,3,2,1,0:T(8,128)(2,1)} %bitcast.7), calls=%async_computation.3 | async-start | bytes 1048576 | tf_op jit(solution)/shard_map/all_to_all | solution.py:335
  166.8 4.9 %join_heads.1 = (bf16[2048,512]{1,0:T(8,128)(2,1)}, bf16[2048,512]{1,0:T(8,128)(2,1)}) custom-call(bf16[4,2,2048,128]{3,2,1,0:T(8,128)(2,1)} %all-to-all-done.2.a_ref), custom_call_target="tpu_custom_call" | custom-call | tf_op jit(solution)/shard_map/join_heads/pallas_call | solution.py:230
  171.8 4.1 %all-to-all-done.3.a_ref = bf16[16,2,2,32,128]{4,3,2,1,0:T(8,128)(2,1)S(1)} async-done(((bf16[16,2,2,32,128]{4,3,2,1,0:T(8,128)(2,1)}), bf16[16,2,2,32,128]{4,3,2,1,0:T(8,128)(2,1)S(1)}, u32[]{:S(2)}, u32[]{:S(2)}) %all-to-all-start.3) | async-done | bytes 524320 | tf_op jit(solution)/shard_map/all_to_all | solution.py:335
  (140 shorter events, 52.5 us)
Async XLA Ops:
  2.5 18.1 %all-to-all-start.1 = ((bf16[16,2,2,32,128]{4,3,2,1,0:T(8,128)(2,1)}), bf16[16,2,2,32,128]{4,3,2,1,0:T(8,128)(2,1)S(1)}, u32[]{:S(2)}, u32[]{:S(2)}) async-start(bf16[16,2,2,32,128]{4,3,2,1,0:T(8,128)(2,1)} %pack_encodings.1), calls=%async_computation.1 | async-start | bytes 1048576 | tf_op jit(solution)/shard_map/all_to_all | solution.py:295
  20.6 63.0 %all-to-all-start = ((bf16[4,2,2048,128]{3,2,1,0:T(8,128)(2,1)}), bf16[4,2,2048,128]{3,2,1,0:T(8,128)(2,1)}, u32[]{:S(2)}, u32[]{:S(2)}) async-start(bf16[4,2,2048,128]{3,2,1,0:T(8,128)(2,1)} %split_heads.1), calls=%async_computation | async-start | bytes 8388608 | tf_op jit(solution)/shard_map/all_to_all | solution.py:300
  34.9 11.2 %collective-permute-start.3 = (bf16[8,128,128]{2,1,0:T(8,128)(2,1)S(1)}, bf16[8,128,128]{2,1,0:T(8,128)(2,1)S(1)}, u32[]{:S(2)}, u32[]{:S(2)}) collective-permute-start(bf16[8,128,128]{2,1,0:T(8,128)(2,1)S(1)} %collective-permute-done.1), channel_id=1, source_target_pairs={{0,56},{8,0},{16,8},{24,16},{32,24},{40,32},{48,40},{56,48},{1,57}... | collective-permute-start | bytes 786440 | tf_op jit(solution)/shard_map/ppermute | solution.py:32
  38.4 11.2 %collective-permute-start.2 = (bf16[8,128,128]{2,1,0:T(8,128)(2,1)S(1)}, bf16[8,128,128]{2,1,0:T(8,128)(2,1)S(1)}, u32[]{:S(2)}, u32[]{:S(2)}) collective-permute-start(bf16[8,128,128]{2,1,0:T(8,128)(2,1)S(1)} %collective-permute-done), channel_id=1, source_target_pairs={{0,8},{8,16},{16,24},{24,32},{32,40},{40,48},{48,56},{56,0},{1,9},... | collective-permute-start | bytes 786440 | tf_op jit(solution)/shard_map/ppermute | solution.py:32
  40.5 11.2 %collective-permute-start.13 = (bf16[8,128,128]{2,1,0:T(8,128)(2,1)S(1)}, bf16[8,128,128]{2,1,0:T(8,128)(2,1)S(1)}, u32[]{:S(2)}, u32[]{:S(2)}) collective-permute-start(bf16[8,128,128]{2,1,0:T(8,128)(2,1)S(1)} %collective-permute-done.11), channel_id=1, source_target_pairs={{0,56},{8,0},{16,8},{24,16},{32,24},{40,32},{48,40},{56,48},{1,57}... | collective-permute-start | bytes 786440 | tf_op jit(solution)/shard_map/ppermute | solution.py:32
  44.0 11.2 %collective-permute-start.12 = (bf16[8,128,128]{2,1,0:T(8,128)(2,1)S(1)}, bf16[8,128,128]{2,1,0:T(8,128)(2,1)S(1)}, u32[]{:S(2)}, u32[]{:S(2)}) collective-permute-start(bf16[8,128,128]{2,1,0:T(8,128)(2,1)S(1)} %collective-permute-done.10), channel_id=1, source_target_pairs={{0,8},{8,16},{16,24},{24,32},{32,40},{40,48},{48,56},{56,0},{1,9},... | collective-permute-start | bytes 786440 | tf_op jit(solution)/shard_map/ppermute | solution.py:32
  46.1 15.0 %collective-permute-start.5 = (bf16[8,128,128]{2,1,0:T(8,128)(2,1)S(1)}, bf16[8,128,128]{2,1,0:T(8,128)(2,1)S(1)}, u32[]{:S(2)}, u32[]{:S(2)}) collective-permute-start(bf16[8,128,128]{2,1,0:T(8,128)(2,1)S(1)} %collective-permute-done.3), channel_id=1, source_target_pairs={{0,56},{8,0},{16,8},{24,16},{32,24},{40,32},{48,40},{56,48},{1,57}... | collective-permute-start | bytes 786440 | tf_op jit(solution)/shard_map/ppermute | solution.py:32
  49.7 13.1 %collective-permute-start.4 = (bf16[8,128,128]{2,1,0:T(8,128)(2,1)S(1)}, bf16[8,128,128]{2,1,0:T(8,128)(2,1)S(1)}, u32[]{:S(2)}, u32[]{:S(2)}) collective-permute-start(bf16[8,128,128]{2,1,0:T(8,128)(2,1)S(1)} %collective-permute-done.2), channel_id=1, source_target_pairs={{0,8},{8,16},{16,24},{24,32},{32,40},{40,48},{48,56},{56,0},{1,9},... | collective-permute-start | bytes 786440 | tf_op jit(solution)/shard_map/ppermute | solution.py:32
  51.8 14.7 %collective-permute-start.15 = (bf16[8,128,128]{2,1,0:T(8,128)(2,1)S(1)}, bf16[8,128,128]{2,1,0:T(8,128)(2,1)S(1)}, u32[]{:S(2)}, u32[]{:S(2)}) collective-permute-start(bf16[8,128,128]{2,1,0:T(8,128)(2,1)S(1)} %collective-permute-done.13), channel_id=1, source_target_pairs={{0,56},{8,0},{16,8},{24,16},{32,24},{40,32},{48,40},{56,48},{1,57}... | collective-permute-start | bytes 786440 | tf_op jit(solution)/shard_map/ppermute | solution.py:32
  55.4 28.2 %collective-permute-start.18 = (bf16[40,128,128]{2,1,0:T(8,128)(2,1)S(1)}, bf16[40,128,128]{2,1,0:T(8,128)(2,1)}, u32[]{:S(2)}, u32[]{:S(2)}) collective-permute-start(bf16[40,128,128]{2,1,0:T(8,128)(2,1)S(1)} %constant_dynamic-update-slice_fusion.9.refs_4_), channel_id=1, source_target_pairs={{0,4},{4,0},{1,5},{5,1},{2,6},{6,2},{3,7},{7,3},{8,12},{12,8},{9,1... | collective-permute-start | bytes 3932168 | tf_op jit(solution)/shard_map/ppermute | solution.py:32
  61.1 22.5 %collective-permute-start.8 = (bf16[40,128,128]{2,1,0:T(8,128)(2,1)S(1)}, bf16[40,128,128]{2,1,0:T(8,128)(2,1)}, u32[]{:S(2)}, u32[]{:S(2)}) collective-permute-start(bf16[40,128,128]{2,1,0:T(8,128)(2,1)S(1)} %constant_dynamic-update-slice_fusion.refs_0_), channel_id=1, source_target_pairs={{0,4},{4,0},{1,5},{5,1},{2,6},{6,2},{3,7},{7,3},{8,12},{12,8},{9,1... | collective-permute-start | bytes 3932168 | tf_op jit(solution)/shard_map/ppermute | solution.py:32
  62.8 10.5 %collective-permute-start.7 = (bf16[4,128,128]{2,1,0:T(8,128)(2,1)S(1)}, bf16[4,128,128]{2,1,0:T(8,128)(2,1)S(1)}, u32[]{:S(2)}, u32[]{:S(2)}) collective-permute-start(bf16[4,128,128]{2,1,0:T(8,128)(2,1)S(1)} %slice.188), channel_id=1, source_target_pairs={{0,56},{8,0},{16,8},{24,16},{32,24},{40,32},{48,40},{56,48},{1,57}... | collective-permute-start | bytes 393224 | tf_op jit(solution)/shard_map/ppermute | solution.py:32
  104.9 57.2 %all-to-all-start.2 = ((bf16[4,2,2048,128]{3,2,1,0:T(8,128)(2,1)}), bf16[4,2,2048,128]{3,2,1,0:T(8,128)(2,1)}, u32[]{:S(2)}, u32[]{:S(2)}) async-start(bf16[4,2,2048,128]{3,2,1,0:T(8,128)(2,1)} %get-tuple-element.23), calls=%async_computation.2 | async-start | bytes 8388608 | tf_op jit(solution)/shard_map/all_to_all | solution.py:318
  109.9 19.2 %collective-permute-start.20 = (bf16[40,128,128]{2,1,0:T(8,128)(2,1)}, bf16[40,128,128]{2,1,0:T(8,128)(2,1)S(1)}, u32[]{:S(2)}, u32[]{:S(2)}) collective-permute-start(bf16[40,128,128]{2,1,0:T(8,128)(2,1)} %get-tuple-element.18), channel_id=1, source_target_pairs={{0,4},{4,0},{1,5},{5,1},{2,6},{6,2},{3,7},{7,3},{8,12},{12,8},{9,1... | collective-permute-start | bytes 3932168 | tf_op jit(solution)/shard_map/ppermute | solution.py:32
  110.4 25.3 %collective-permute-start.30 = (bf16[40,128,128]{2,1,0:T(8,128)(2,1)}, bf16[40,128,128]{2,1,0:T(8,128)(2,1)S(1)}, u32[]{:S(2)}, u32[]{:S(2)}) collective-permute-start(bf16[40,128,128]{2,1,0:T(8,128)(2,1)} %get-tuple-element.21), channel_id=1, source_target_pairs={{0,4},{4,0},{1,5},{5,1},{2,6},{6,2},{3,7},{7,3},{8,12},{12,8},{9,1... | collective-permute-start | bytes 3932168 | tf_op jit(solution)/shard_map/ppermute | solution.py:32
  118.2 10.8 %collective-permute-start.23 = (bf16[8,128,128]{2,1,0:T(8,128)(2,1)S(1)}, bf16[8,128,128]{2,1,0:T(8,128)(2,1)S(1)}, u32[]{:S(2)}, u32[]{:S(2)}) collective-permute-start(bf16[8,128,128]{2,1,0:T(8,128)(2,1)S(1)} %pad_maximum_fusion), channel_id=1, source_target_pairs={{0,8},{8,16},{16,24},{24,32},{32,40},{40,48},{48,56},{56,0},{1,9},... | collective-permute-start | bytes 786440 | tf_op jit(solution)/shard_map/ppermute | solution.py:32
  123.6 10.9 %collective-permute-start.33 = (bf16[8,128,128]{2,1,0:T(8,128)(2,1)S(1)}, bf16[8,128,128]{2,1,0:T(8,128)(2,1)S(1)}, u32[]{:S(2)}, u32[]{:S(2)}) collective-permute-start(bf16[8,128,128]{2,1,0:T(8,128)(2,1)S(1)} %pad_maximum_fusion.2), channel_id=1, source_target_pairs={{0,8},{8,16},{16,24},{24,32},{32,40},{40,48},{48,56},{56,0},{1,9},... | collective-permute-start | bytes 786440 | tf_op jit(solution)/shard_map/ppermute | solution.py:32
  129.2 12.0 %collective-permute-start.28 = (bf16[8,128,128]{2,1,0:T(8,128)(2,1)S(1)}, bf16[8,128,128]{2,1,0:T(8,128)(2,1)S(1)}, u32[]{:S(2)}, u32[]{:S(2)}) collective-permute-start(bf16[8,128,128]{2,1,0:T(8,128)(2,1)S(1)} %get-tuple-element.36), channel_id=1, source_target_pairs={{0,56},{8,0},{16,8},{24,16},{32,24},{40,32},{48,40},{56,48},{1,57}... | collective-permute-start | bytes 786440 | tf_op jit(solution)/shard_map/ppermute | solution.py:32
  130.5 10.8 %collective-permute-start.24 = (bf16[8,128,128]{2,1,0:T(8,128)(2,1)S(1)}, bf16[8,128,128]{2,1,0:T(8,128)(2,1)S(1)}, u32[]{:S(2)}, u32[]{:S(2)}) collective-permute-start(bf16[8,128,128]{2,1,0:T(8,128)(2,1)S(1)} %get-tuple-element.37), channel_id=1, source_target_pairs={{0,8},{8,16},{16,24},{24,32},{32,40},{40,48},{48,56},{56,0},{1,9},... | collective-permute-start | bytes 786440 | tf_op jit(solution)/shard_map/ppermute | solution.py:32
  135.8 11.1 %collective-permute-start.38 = (bf16[8,128,128]{2,1,0:T(8,128)(2,1)S(1)}, bf16[8,128,128]{2,1,0:T(8,128)(2,1)S(1)}, u32[]{:S(2)}, u32[]{:S(2)}) collective-permute-start(bf16[8,128,128]{2,1,0:T(8,128)(2,1)S(1)} %get-tuple-element.32), channel_id=1, source_target_pairs={{0,56},{8,0},{16,8},{24,16},{32,24},{40,32},{48,40},{56,48},{1,57}... | collective-permute-start | bytes 786440 | tf_op jit(solution)/shard_map/ppermute | solution.py:32
  136.6 10.3 %collective-permute-start.34 = (bf16[8,128,128]{2,1,0:T(8,128)(2,1)S(1)}, bf16[8,128,128]{2,1,0:T(8,128)(2,1)S(1)}, u32[]{:S(2)}, u32[]{:S(2)}) collective-permute-start(bf16[8,128,128]{2,1,0:T(8,128)(2,1)S(1)} %get-tuple-element.33), channel_id=1, source_target_pairs={{0,8},{8,16},{16,24},{24,32},{32,40},{40,48},{48,56},{56,0},{1,9},... | collective-permute-start | bytes 786440 | tf_op jit(solution)/shard_map/ppermute | solution.py:32
  141.4 11.1 %collective-permute-start.29 = (bf16[8,128,128]{2,1,0:T(8,128)(2,1)S(1)}, bf16[8,128,128]{2,1,0:T(8,128)(2,1)S(1)}, u32[]{:S(2)}, u32[]{:S(2)}) collective-permute-start(bf16[8,128,128]{2,1,0:T(8,128)(2,1)S(1)} %get-tuple-element.34), channel_id=1, source_target_pairs={{0,56},{8,0},{16,8},{24,16},{32,24},{40,32},{48,40},{56,48},{1,57}... | collective-permute-start | bytes 786440 | tf_op jit(solution)/shard_map/ppermute | solution.py:32
  147.0 11.1 %collective-permute-start.39 = (bf16[8,128,128]{2,1,0:T(8,128)(2,1)S(1)}, bf16[8,128,128]{2,1,0:T(8,128)(2,1)S(1)}, u32[]{:S(2)}, u32[]{:S(2)}) collective-permute-start(bf16[8,128,128]{2,1,0:T(8,128)(2,1)S(1)} %get-tuple-element.30), channel_id=1, source_target_pairs={{0,56},{8,0},{16,8},{24,16},{32,24},{40,32},{48,40},{56,48},{1,57}... | collective-permute-start | bytes 786440 | tf_op jit(solution)/shard_map/ppermute | solution.py:32
  162.1 13.8 %all-to-all-start.3 = ((bf16[16,2,2,32,128]{4,3,2,1,0:T(8,128)(2,1)}), bf16[16,2,2,32,128]{4,3,2,1,0:T(8,128)(2,1)S(1)}, u32[]{:S(2)}, u32[]{:S(2)}) async-start(bf16[16,2,2,32,128]{4,3,2,1,0:T(8,128)(2,1)} %bitcast.7), calls=%async_computation.3 | async-start | bytes 1048576 | tf_op jit(solution)/shard_map/all_to_all | solution.py:335
  (33 other events, 245.4 us)
where the time goes:
time: 182 us; the launch traced here: 179 us
  starting transfers between devices  71.7 us (39%)
  waiting for transfers between devices  60.7 us (33%)
  Pallas kernels  37 us (20%)
  local copies, waits for them, and re-layouts  5.82 us (3%)
  other arithmetic  2.49 us (1%)
    ppermute x40, waiting for transfers between devices, shift(): return lax.ppermute(a, axis, [(i, (i + by) % size) for i in range(size)])  51 us
    ppermute x40, starting transfers between devices, shift(): return lax.ppermute(a, axis, [(i, (i + by) % size) for i in range(size)])  49.5 us
    pallas_call x1, Pallas kernels, attention(): pl.pallas_call(attention_kernel, grid_spec=pltpu.PrefetchScalarGridSpec(n...  20.7 us
    all_to_all x1, starting transfers between devices, per_device(): lax.all_to_all(both, ('head', 'x'), split_axis=0, concat_axis=0, tiled=True)  7.58 us
    all_to_all x1, waiting for transfers between devices, per_device(): lax.all_to_all(both, ('head', 'x'), split_axis=0, concat_axis=0, tiled=True)  5.6 us
    all_to_all x1, starting transfers between devices, per_device(): reply = lax.all_to_all(reply, 'x', split_axis=0, concat_axis=0, tiled=True)  5 us
    pallas_call x1, Pallas kernels, join_heads(): pl.pallas_call(kernel, grid=(tokens // rows,), in_specs=[pl.BlockSpec((X,...  4.94 us
    pallas_call x1, Pallas kernels, split_heads(): pl.pallas_call(kernel, grid=(tokens // rows,), in_specs=[wide, wide], out...  4.91 us
  transfers between devices with their start and end apart: 44, of which 20 were waited for; matrix products, arithmetic and copies ran while one was open for 3% of the time, Pallas kernels for 7%

commit v1 on v0

--- a/solution.py
+++ b/solution.py
@@ -24,7 +24,7 @@
 EARLY, LATE = (0, 7, 1, 6, 2), (5, 3, 4)
 ORDER = EARLY + LATE
 N_EARLY, N_LATE = len(EARLY) * GROUP, len(LATE) * GROUP
-BATCH = 16
+BATCH = 32
 MIB = 1024 * 1024
 
 

time: 182 us -> 181 us (level)
  no operation moved by 1% of the time
where the time goes in v1:
time: 181 us; the launch traced here: 178 us
  starting transfers between devices  71.9 us (40%)
  waiting for transfers between devices  60.5 us (33%)
  Pallas kernels  36 us (20%)
  local copies, waits for them, and re-layouts  5.82 us (3%)
  other arithmetic  2.49 us (1%)
    ppermute x40, waiting for transfers between devices, shift(): return lax.ppermute(a, axis, [(i, (i + by) % size) for i in range(size)])  50.7 us
    ppermute x40, starting transfers between devices, shift(): return lax.ppermute(a, axis, [(i, (i + by) % size) for i in range(size)])  49.7 us
    pallas_call x1, Pallas kernels, attention(): pl.pallas_call(attention_kernel, grid_spec=pltpu.PrefetchScalarGridSpec(n...  19.7 us
    all_to_all x1, starting transfers between devices, per_device(): lax.all_to_all(both, ('head', 'x'), split_axis=0, concat_axis=0, tiled=True)  7.58 us
    all_to_all x1, waiting for transfers between devices, per_device(): lax.all_to_all(both, ('head', 'x'), split_axis=0, concat_axis=0, tiled=True)  5.6 us
    all_to_all x1, starting transfers between devices, per_device(): reply = lax.all_to_all(reply, 'x', split_axis=0, concat_axis=0, tiled=True)  5 us
    pallas_call x1, Pallas kernels, join_heads(): pl.pallas_call(kernel, grid=(tokens // rows,), in_specs=[pl.BlockSpec((X,...  4.94 us
    pallas_call x1, Pallas kernels, split_heads(): pl.pallas_call(kernel, grid=(tokens // rows,), in_specs=[wide, wide], out...  4.91 us
  transfers between devices with their start and end apart: 44, of which 20 were waited for; matrix products, arithmetic and copies ran while one was open for 3% of the time, Pallas kernels for 7%

profile of v1, /device:TPU:1, one launch (start us, length us, event | category | flops | bytes accessed | tf_op | source)
XLA Modules:
  0.0 177.7 jit_solution(11386441090415645409)
XLA Ops:
  2.5 7.6 %all-to-all-start.1 = ((bf16[16,2,2,32,128]{4,3,2,1,0:T(8,128)(2,1)}), bf16[16,2,2,32,128]{4,3,2,1,0:T(8,128)(2,1)S(1)}, u32[]{:S(2)}, u32[]{:S(2)}) async-start(bf16[16,2,2,32,128]{4,3,2,1,0:T(8,128)(2,1)} %pack_encodings.1), calls=%async_computation.1 | async-start | bytes 1048576 | tf_op jit(solution)/shard_map/all_to_all | solution.py:295
  10.1 4.9 %split_heads.1 = bf16[4,2,2048,128]{3,2,1,0:T(8,128)(2,1)} custom-call(bf16[2048,512]{1,0:T(8,128)(2,1)} %a_ref.1, bf16[2048,512]{1,0:T(8,128)(2,1)} %b_ref.1), custom_call_target="tpu_custom_call" | custom-call | tf_op jit(solution)/shard_map/split_heads/pallas_call | solution.py:209
  15.1 5.6 %all-to-all-done.1 = bf16[16,2,2,32,128]{4,3,2,1,0:T(8,128)(2,1)S(1)} async-done(((bf16[16,2,2,32,128]{4,3,2,1,0:T(8,128)(2,1)}), bf16[16,2,2,32,128]{4,3,2,1,0:T(8,128)(2,1)S(1)}, u32[]{:S(2)}, u32[]{:S(2)}) %all-to-all-start.1) | async-done | bytes 524320 | tf_op jit(solution)/shard_map/all_to_all | solution.py:295
  20.6 4.9 %all-to-all-start = ((bf16[4,2,2048,128]{3,2,1,0:T(8,128)(2,1)}), bf16[4,2,2048,128]{3,2,1,0:T(8,128)(2,1)}, u32[]{:S(2)}, u32[]{:S(2)}) async-start(bf16[4,2,2048,128]{3,2,1,0:T(8,128)(2,1)} %split_heads.1), calls=%async_computation | async-start | bytes 8388608 | tf_op jit(solution)/shard_map/all_to_all | solution.py:300
  25.6 5.7 %collective-permute-start.1 = (bf16[8,128,128]{2,1,0:T(8,128)(2,1)S(1)}, bf16[8,128,128]{2,1,0:T(8,128)(2,1)S(1)}, u32[]{:S(2)}, u32[]{:S(2)}) collective-permute-start(bf16[8,128,128]{2,1,0:T(8,128)(2,1)S(1)} %bitcast.13), channel_id=1, source_target_pairs={{0,56},{8,0},{16,8},{24,16},{32,24},{40,32},{48,40},{56,48},{1,57}... | collective-permute-start | bytes 786440 | tf_op jit(solution)/shard_map/ppermute | solution.py:32
  34.9 3.5 %collective-permute-start.3 = (bf16[8,128,128]{2,1,0:T(8,128)(2,1)S(1)}, bf16[8,128,128]{2,1,0:T(8,128)(2,1)S(1)}, u32[]{:S(2)}, u32[]{:S(2)}) collective-permute-start(bf16[8,128,128]{2,1,0:T(8,128)(2,1)S(1)} %collective-permute-done.1), channel_id=1, source_target_pairs={{0,56},{8,0},{16,8},{24,16},{32,24},{40,32},{48,40},{56,48},{1,57}... | collective-permute-start | bytes 786440 | tf_op jit(solution)/shard_map/ppermute | solution.py:32
  40.5 3.5 %collective-permute-start.13 = (bf16[8,128,128]{2,1,0:T(8,128)(2,1)S(1)}, bf16[8,128,128]{2,1,0:T(8,128)(2,1)S(1)}, u32[]{:S(2)}, u32[]{:S(2)}) collective-permute-start(bf16[8,128,128]{2,1,0:T(8,128)(2,1)S(1)} %collective-permute-done.11), channel_id=1, source_target_pairs={{0,56},{8,0},{16,8},{24,16},{32,24},{40,32},{48,40},{56,48},{1,57}... | collective-permute-start | bytes 786440 | tf_op jit(solution)/shard_map/ppermute | solution.py:32
  46.1 3.5 %collective-permute-start.5 = (bf16[8,128,128]{2,1,0:T(8,128)(2,1)S(1)}, bf16[8,128,128]{2,1,0:T(8,128)(2,1)S(1)}, u32[]{:S(2)}, u32[]{:S(2)}) collective-permute-start(bf16[8,128,128]{2,1,0:T(8,128)(2,1)S(1)} %collective-permute-done.3), channel_id=1, source_target_pairs={{0,56},{8,0},{16,8},{24,16},{32,24},{40,32},{48,40},{56,48},{1,57}... | collective-permute-start | bytes 786440 | tf_op jit(solution)/shard_map/ppermute | solution.py:32
  51.8 3.5 %collective-permute-start.15 = (bf16[8,128,128]{2,1,0:T(8,128)(2,1)S(1)}, bf16[8,128,128]{2,1,0:T(8,128)(2,1)S(1)}, u32[]{:S(2)}, u32[]{:S(2)}) collective-permute-start(bf16[8,128,128]{2,1,0:T(8,128)(2,1)S(1)} %collective-permute-done.13), channel_id=1, source_target_pairs={{0,56},{8,0},{16,8},{24,16},{32,24},{40,32},{48,40},{56,48},{1,57}... | collective-permute-start | bytes 786440 | tf_op jit(solution)/shard_map/ppermute | solution.py:32
  55.4 5.7 %collective-permute-start.18 = (bf16[40,128,128]{2,1,0:T(8,128)(2,1)S(1)}, bf16[40,128,128]{2,1,0:T(8,128)(2,1)}, u32[]{:S(2)}, u32[]{:S(2)}) collective-permute-start(bf16[40,128,128]{2,1,0:T(8,128)(2,1)S(1)} %constant_dynamic-update-slice_fusion.9.refs_4_), channel_id=1, source_target_pairs={{0,4},{4,0},{1,5},{5,1},{2,6},{6,2},{3,7},{7,3},{8,12},{12,8},{9,1... | collective-permute-start | bytes 3932168 | tf_op jit(solution)/shard_map/ppermute | solution.py:32
  62.8 3.7 %collective-permute-start.7 = (bf16[4,128,128]{2,1,0:T(8,128)(2,1)S(1)}, bf16[4,128,128]{2,1,0:T(8,128)(2,1)S(1)}, u32[]{:S(2)}, u32[]{:S(2)}) collective-permute-start(bf16[4,128,128]{2,1,0:T(8,128)(2,1)S(1)} %slice.188), channel_id=1, source_target_pairs={{0,56},{8,0},{16,8},{24,16},{32,24},{40,32},{48,40},{56,48},{1,57}... | collective-permute-start | bytes 393224 | tf_op jit(solution)/shard_map/ppermute | solution.py:32
  66.6 3.6 %collective-permute-done.14 = bf16[8,128,128]{2,1,0:T(8,128)(2,1)S(1)} collective-permute-done((bf16[8,128,128]{2,1,0:T(8,128)(2,1)S(1)}, bf16[8,128,128]{2,1,0:T(8,128)(2,1)S(1)}, u32[]{:S(2)}, u32[]{:S(2)}) %collective-permute-start.14) | collective-permute-done | bytes 262176 | tf_op jit(solution)/shard_map/ppermute | solution.py:32
  83.6 19.7 %attention.1 = (bf16[4,2,2048,128]{3,2,1,0:T(8,128)(2,1)}, bf16[24,128,128]{2,1,0:T(8,128)(2,1)}, bf16[40,128,128]{2,1,0:T(8,128)(2,1)}, bf16[64,128,128]{2,1,0:...) custom-call(s32[128]{0:T(128)} %fusion.8.ids, ...), custom_call_target="tpu_custom_call" | custom-call | tf_op jit(solution)/shard_map/attention/pallas_call | solution.py:171
  103.9 5.0 %all-to-all-start.2 = ((bf16[4,2,2048,128]{3,2,1,0:T(8,128)(2,1)}), bf16[4,2,2048,128]{3,2,1,0:T(8,128)(2,1)}, u32[]{:S(2)}, u32[]{:S(2)}) async-start(bf16[4,2,2048,128]{3,2,1,0:T(8,128)(2,1)} %get-tuple-element.23), calls=%async_computation.2 | async-start | bytes 8388608 | tf_op jit(solution)/shard_map/all_to_all | solution.py:318
  117.7 4.8 %collective-permute-done.32 = bf16[4,128,128]{2,1,0:T(8,128)(2,1)S(1)} collective-permute-done((bf16[4,128,128]{2,1,0:T(8,128)(2,1)S(1)}, bf16[4,128,128]{2,1,0:T(8,128)(2,1)S(1)}, u32[]{:S(2)}, u32[]{:S(2)}) %collective-permute-start.32) | collective-permute-done | bytes 131104 | tf_op jit(solution)/shard_map/ppermute | solution.py:32
  124.2 3.7 %collective-permute-done.23 = bf16[8,128,128]{2,1,0:T(8,128)(2,1)S(1)} collective-permute-done((bf16[8,128,128]{2,1,0:T(8,128)(2,1)S(1)}, bf16[8,128,128]{2,1,0:T(8,128)(2,1)S(1)}, u32[]{:S(2)}, u32[]{:S(2)}) %collective-permute-start.23) | collective-permute-done | bytes 262176 | tf_op jit(solution)/shard_map/ppermute | solution.py:32
  129.8 3.8 %collective-permute-done.33 = bf16[8,128,128]{2,1,0:T(8,128)(2,1)S(1)} collective-permute-done((bf16[8,128,128]{2,1,0:T(8,128)(2,1)S(1)}, bf16[8,128,128]{2,1,0:T(8,128)(2,1)S(1)}, u32[]{:S(2)}, u32[]{:S(2)}) %collective-permute-start.33) | collective-permute-done | bytes 262176 | tf_op jit(solution)/shard_map/ppermute | solution.py:32
  136.3 3.9 %collective-permute-done.28 = bf16[8,128,128]{2,1,0:T(8,128)(2,1)S(1)} collective-permute-done((bf16[8,128,128]{2,1,0:T(8,128)(2,1)S(1)}, bf16[8,128,128]{2,1,0:T(8,128)(2,1)S(1)}, u32[]{:S(2)}, u32[]{:S(2)}) %collective-permute-start.28) | collective-permute-done | bytes 262176 | tf_op jit(solution)/shard_map/ppermute | solution.py:32
  141.9 4.0 %collective-permute-done.38 = bf16[8,128,128]{2,1,0:T(8,128)(2,1)S(1)} collective-permute-done((bf16[8,128,128]{2,1,0:T(8,128)(2,1)S(1)}, bf16[8,128,128]{2,1,0:T(8,128)(2,1)S(1)}, u32[]{:S(2)}, u32[]{:S(2)}) %collective-permute-start.38) | collective-permute-done | bytes 262176 | tf_op jit(solution)/shard_map/ppermute | solution.py:32
  147.5 4.0 %collective-permute-done.29.refs_3_ = bf16[8,128,128]{2,1,0:T(8,128)(2,1)S(1)} collective-permute-done((bf16[8,128,128]{2,1,0:T(8,128)(2,1)S(1)}, bf16[8,128,128]{2,1,0:T(8,128)(2,1)S(1)}, u32[]{:S(2)}, u32[]{:S(2)}) %collective-permute-start.29) | collective-permute-done | bytes 262176 | tf_op jit(solution)/shard_map/ppermute | solution.py:32
  151.5 5.6 %collective-permute-done.39.refs_7_ = bf16[8,128,128]{2,1,0:T(8,128)(2,1)S(1)} collective-permute-done((bf16[8,128,128]{2,1,0:T(8,128)(2,1)S(1)}, bf16[8,128,128]{2,1,0:T(8,128)(2,1)S(1)}, u32[]{:S(2)}, u32[]{:S(2)}) %collective-permute-start.39) | collective-permute-done | bytes 262176 | tf_op jit(solution)/shard_map/ppermute | solution.py:32
  161.1 4.7 %all-to-all-start.3 = ((bf16[16,2,2,32,128]{4,3,2,1,0:T(8,128)(2,1)}), bf16[16,2,2,32,128]{4,3,2,1,0:T(8,128)(2,1)S(1)}, u32[]{:S(2)}, u32[]{:S(2)}) async-start(bf16[16,2,2,32,128]{4,3,2,1,0:T(8,128)(2,1)} %bitcast.7), calls=%async_computation.3 | async-start | bytes 1048576 | tf_op jit(solution)/shard_map/all_to_all | solution.py:335
  165.8 4.9 %join_heads.1 = (bf16[2048,512]{1,0:T(8,128)(2,1)}, bf16[2048,512]{1,0:T(8,128)(2,1)}) custom-call(bf16[4,2,2048,128]{3,2,1,0:T(8,128)(2,1)} %all-to-all-done.2.a_ref), custom_call_target="tpu_custom_call" | custom-call | tf_op jit(solution)/shard_map/join_heads/pallas_call | solution.py:230
  170.8 4.2 %all-to-all-done.3.a_ref = bf16[16,2,2,32,128]{4,3,2,1,0:T(8,128)(2,1)S(1)} async-done(((bf16[16,2,2,32,128]{4,3,2,1,0:T(8,128)(2,1)}), bf16[16,2,2,32,128]{4,3,2,1,0:T(8,128)(2,1)S(1)}, u32[]{:S(2)}, u32[]{:S(2)}) %all-to-all-start.3) | async-done | bytes 524320 | tf_op jit(solution)/shard_map/all_to_all | solution.py:335
  (140 shorter events, 52.8 us)
Async XLA Ops:
  2.5 18.1 %all-to-all-start.1 = ((bf16[16,2,2,32,128]{4,3,2,1,0:T(8,128)(2,1)}), bf16[16,2,2,32,128]{4,3,2,1,0:T(8,128)(2,1)S(1)}, u32[]{:S(2)}, u32[]{:S(2)}) async-start(bf16[16,2,2,32,128]{4,3,2,1,0:T(8,128)(2,1)} %pack_encodings.1), calls=%async_computation.1 | async-start | bytes 1048576 | tf_op jit(solution)/shard_map/all_to_all | solution.py:295
  20.6 63.0 %all-to-all-start = ((bf16[4,2,2048,128]{3,2,1,0:T(8,128)(2,1)}), bf16[4,2,2048,128]{3,2,1,0:T(8,128)(2,1)}, u32[]{:S(2)}, u32[]{:S(2)}) async-start(bf16[4,2,2048,128]{3,2,1,0:T(8,128)(2,1)} %split_heads.1), calls=%async_computation | async-start | bytes 8388608 | tf_op jit(solution)/shard_map/all_to_all | solution.py:300
  34.9 11.2 %collective-permute-start.3 = (bf16[8,128,128]{2,1,0:T(8,128)(2,1)S(1)}, bf16[8,128,128]{2,1,0:T(8,128)(2,1)S(1)}, u32[]{:S(2)}, u32[]{:S(2)}) collective-permute-start(bf16[8,128,128]{2,1,0:T(8,128)(2,1)S(1)} %collective-permute-done.1), channel_id=1, source_target_pairs={{0,56},{8,0},{16,8},{24,16},{32,24},{40,32},{48,40},{56,48},{1,57}... | collective-permute-start | bytes 786440 | tf_op jit(solution)/shard_map/ppermute | solution.py:32
  38.4 11.2 %collective-permute-start.2 = (bf16[8,128,128]{2,1,0:T(8,128)(2,1)S(1)}, bf16[8,128,128]{2,1,0:T(8,128)(2,1)S(1)}, u32[]{:S(2)}, u32[]{:S(2)}) collective-permute-start(bf16[8,128,128]{2,1,0:T(8,128)(2,1)S(1)} %collective-permute-done), channel_id=1, source_target_pairs={{0,8},{8,16},{16,24},{24,32},{32,40},{40,48},{48,56},{56,0},{1,9},... | collective-permute-start | bytes 786440 | tf_op jit(solution)/shard_map/ppermute | solution.py:32
  40.5 11.2 %collective-permute-start.13 = (bf16[8,128,128]{2,1,0:T(8,128)(2,1)S(1)}, bf16[8,128,128]{2,1,0:T(8,128)(2,1)S(1)}, u32[]{:S(2)}, u32[]{:S(2)}) collective-permute-start(bf16[8,128,128]{2,1,0:T(8,128)(2,1)S(1)} %collective-permute-done.11), channel_id=1, source_target_pairs={{0,56},{8,0},{16,8},{24,16},{32,24},{40,32},{48,40},{56,48},{1,57}... | collective-permute-start | bytes 786440 | tf_op jit(solution)/shard_map/ppermute | solution.py:32
  44.0 11.2 %collective-permute-start.12 = (bf16[8,128,128]{2,1,0:T(8,128)(2,1)S(1)}, bf16[8,128,128]{2,1,0:T(8,128)(2,1)S(1)}, u32[]{:S(2)}, u32[]{:S(2)}) collective-permute-start(bf16[8,128,128]{2,1,0:T(8,128)(2,1)S(1)} %collective-permute-done.10), channel_id=1, source_target_pairs={{0,8},{8,16},{16,24},{24,32},{32,40},{40,48},{48,56},{56,0},{1,9},... | collective-permute-start | bytes 786440 | tf_op jit(solution)/shard_map/ppermute | solution.py:32
  46.1 15.0 %collective-permute-start.5 = (bf16[8,128,128]{2,1,0:T(8,128)(2,1)S(1)}, bf16[8,128,128]{2,1,0:T(8,128)(2,1)S(1)}, u32[]{:S(2)}, u32[]{:S(2)}) collective-permute-start(bf16[8,128,128]{2,1,0:T(8,128)(2,1)S(1)} %collective-permute-done.3), channel_id=1, source_target_pairs={{0,56},{8,0},{16,8},{24,16},{32,24},{40,32},{48,40},{56,48},{1,57}... | collective-permute-start | bytes 786440 | tf_op jit(solution)/shard_map/ppermute | solution.py:32
  49.7 13.1 %collective-permute-start.4 = (bf16[8,128,128]{2,1,0:T(8,128)(2,1)S(1)}, bf16[8,128,128]{2,1,0:T(8,128)(2,1)S(1)}, u32[]{:S(2)}, u32[]{:S(2)}) collective-permute-start(bf16[8,128,128]{2,1,0:T(8,128)(2,1)S(1)} %collective-permute-done.2), channel_id=1, source_target_pairs={{0,8},{8,16},{16,24},{24,32},{32,40},{40,48},{48,56},{56,0},{1,9},... | collective-permute-start | bytes 786440 | tf_op jit(solution)/shard_map/ppermute | solution.py:32
  51.8 14.7 %collective-permute-start.15 = (bf16[8,128,128]{2,1,0:T(8,128)(2,1)S(1)}, bf16[8,128,128]{2,1,0:T(8,128)(2,1)S(1)}, u32[]{:S(2)}, u32[]{:S(2)}) collective-permute-start(bf16[8,128,128]{2,1,0:T(8,128)(2,1)S(1)} %collective-permute-done.13), channel_id=1, source_target_pairs={{0,56},{8,0},{16,8},{24,16},{32,24},{40,32},{48,40},{56,48},{1,57}... | collective-permute-start | bytes 786440 | tf_op jit(solution)/shard_map/ppermute | solution.py:32
  55.4 28.2 %collective-permute-start.18 = (bf16[40,128,128]{2,1,0:T(8,128)(2,1)S(1)}, bf16[40,128,128]{2,1,0:T(8,128)(2,1)}, u32[]{:S(2)}, u32[]{:S(2)}) collective-permute-start(bf16[40,128,128]{2,1,0:T(8,128)(2,1)S(1)} %constant_dynamic-update-slice_fusion.9.refs_4_), channel_id=1, source_target_pairs={{0,4},{4,0},{1,5},{5,1},{2,6},{6,2},{3,7},{7,3},{8,12},{12,8},{9,1... | collective-permute-start | bytes 3932168 | tf_op jit(solution)/shard_map/ppermute | solution.py:32
  61.1 22.5 %collective-permute-start.8 = (bf16[40,128,128]{2,1,0:T(8,128)(2,1)S(1)}, bf16[40,128,128]{2,1,0:T(8,128)(2,1)}, u32[]{:S(2)}, u32[]{:S(2)}) collective-permute-start(bf16[40,128,128]{2,1,0:T(8,128)(2,1)S(1)} %constant_dynamic-update-slice_fusion.refs_0_), channel_id=1, source_target_pairs={{0,4},{4,0},{1,5},{5,1},{2,6},{6,2},{3,7},{7,3},{8,12},{12,8},{9,1... | collective-permute-start | bytes 3932168 | tf_op jit(solution)/shard_map/ppermute | solution.py:32
  62.8 10.5 %collective-permute-start.7 = (bf16[4,128,128]{2,1,0:T(8,128)(2,1)S(1)}, bf16[4,128,128]{2,1,0:T(8,128)(2,1)S(1)}, u32[]{:S(2)}, u32[]{:S(2)}) collective-permute-start(bf16[4,128,128]{2,1,0:T(8,128)(2,1)S(1)} %slice.188), channel_id=1, source_target_pairs={{0,56},{8,0},{16,8},{24,16},{32,24},{40,32},{48,40},{56,48},{1,57}... | collective-permute-start | bytes 393224 | tf_op jit(solution)/shard_map/ppermute | solution.py:32
  103.9 57.2 %all-to-all-start.2 = ((bf16[4,2,2048,128]{3,2,1,0:T(8,128)(2,1)}), bf16[4,2,2048,128]{3,2,1,0:T(8,128)(2,1)}, u32[]{:S(2)}, u32[]{:S(2)}) async-start(bf16[4,2,2048,128]{3,2,1,0:T(8,128)(2,1)} %get-tuple-element.23), calls=%async_computation.2 | async-start | bytes 8388608 | tf_op jit(solution)/shard_map/all_to_all | solution.py:318
  108.9 19.2 %collective-permute-start.20 = (bf16[40,128,128]{2,1,0:T(8,128)(2,1)}, bf16[40,128,128]{2,1,0:T(8,128)(2,1)S(1)}, u32[]{:S(2)}, u32[]{:S(2)}) collective-permute-start(bf16[40,128,128]{2,1,0:T(8,128)(2,1)} %get-tuple-element.18), channel_id=1, source_target_pairs={{0,4},{4,0},{1,5},{5,1},{2,6},{6,2},{3,7},{7,3},{8,12},{12,8},{9,1... | collective-permute-start | bytes 3932168 | tf_op jit(solution)/shard_map/ppermute | solution.py:32
  109.4 25.4 %collective-permute-start.30 = (bf16[40,128,128]{2,1,0:T(8,128)(2,1)}, bf16[40,128,128]{2,1,0:T(8,128)(2,1)S(1)}, u32[]{:S(2)}, u32[]{:S(2)}) collective-permute-start(bf16[40,128,128]{2,1,0:T(8,128)(2,1)} %get-tuple-element.21), channel_id=1, source_target_pairs={{0,4},{4,0},{1,5},{5,1},{2,6},{6,2},{3,7},{7,3},{8,12},{12,8},{9,1... | collective-permute-start | bytes 3932168 | tf_op jit(solution)/shard_map/ppermute | solution.py:32
  117.1 10.8 %collective-permute-start.23 = (bf16[8,128,128]{2,1,0:T(8,128)(2,1)S(1)}, bf16[8,128,128]{2,1,0:T(8,128)(2,1)S(1)}, u32[]{:S(2)}, u32[]{:S(2)}) collective-permute-start(bf16[8,128,128]{2,1,0:T(8,128)(2,1)S(1)} %pad_maximum_fusion), channel_id=1, source_target_pairs={{0,8},{8,16},{16,24},{24,32},{32,40},{40,48},{48,56},{56,0},{1,9},... | collective-permute-start | bytes 786440 | tf_op jit(solution)/shard_map/ppermute | solution.py:32
  122.6 10.9 %collective-permute-start.33 = (bf16[8,128,128]{2,1,0:T(8,128)(2,1)S(1)}, bf16[8,128,128]{2,1,0:T(8,128)(2,1)S(1)}, u32[]{:S(2)}, u32[]{:S(2)}) collective-permute-start(bf16[8,128,128]{2,1,0:T(8,128)(2,1)S(1)} %pad_maximum_fusion.2), channel_id=1, source_target_pairs={{0,8},{8,16},{16,24},{24,32},{32,40},{40,48},{48,56},{56,0},{1,9},... | collective-permute-start | bytes 786440 | tf_op jit(solution)/shard_map/ppermute | solution.py:32
  128.2 12.0 %collective-permute-start.28 = (bf16[8,128,128]{2,1,0:T(8,128)(2,1)S(1)}, bf16[8,128,128]{2,1,0:T(8,128)(2,1)S(1)}, u32[]{:S(2)}, u32[]{:S(2)}) collective-permute-start(bf16[8,128,128]{2,1,0:T(8,128)(2,1)S(1)} %get-tuple-element.36), channel_id=1, source_target_pairs={{0,56},{8,0},{16,8},{24,16},{32,24},{40,32},{48,40},{56,48},{1,57}... | collective-permute-start | bytes 786440 | tf_op jit(solution)/shard_map/ppermute | solution.py:32
  129.5 10.8 %collective-permute-start.24 = (bf16[8,128,128]{2,1,0:T(8,128)(2,1)S(1)}, bf16[8,128,128]{2,1,0:T(8,128)(2,1)S(1)}, u32[]{:S(2)}, u32[]{:S(2)}) collective-permute-start(bf16[8,128,128]{2,1,0:T(8,128)(2,1)S(1)} %get-tuple-element.37), channel_id=1, source_target_pairs={{0,8},{8,16},{16,24},{24,32},{32,40},{40,48},{48,56},{56,0},{1,9},... | collective-permute-start | bytes 786440 | tf_op jit(solution)/shard_map/ppermute | solution.py:32
  134.8 11.1 %collective-permute-start.38 = (bf16[8,128,128]{2,1,0:T(8,128)(2,1)S(1)}, bf16[8,128,128]{2,1,0:T(8,128)(2,1)S(1)}, u32[]{:S(2)}, u32[]{:S(2)}) collective-permute-start(bf16[8,128,128]{2,1,0:T(8,128)(2,1)S(1)} %get-tuple-element.32), channel_id=1, source_target_pairs={{0,56},{8,0},{16,8},{24,16},{32,24},{40,32},{48,40},{56,48},{1,57}... | collective-permute-start | bytes 786440 | tf_op jit(solution)/shard_map/ppermute | solution.py:32
  135.6 10.3 %collective-permute-start.34 = (bf16[8,128,128]{2,1,0:T(8,128)(2,1)S(1)}, bf16[8,128,128]{2,1,0:T(8,128)(2,1)S(1)}, u32[]{:S(2)}, u32[]{:S(2)}) collective-permute-start(bf16[8,128,128]{2,1,0:T(8,128)(2,1)S(1)} %get-tuple-element.33), channel_id=1, source_target_pairs={{0,8},{8,16},{16,24},{24,32},{32,40},{40,48},{48,56},{56,0},{1,9},... | collective-permute-start | bytes 786440 | tf_op jit(solution)/shard_map/ppermute | solution.py:32
  140.3 11.1 %collective-permute-start.29 = (bf16[8,128,128]{2,1,0:T(8,128)(2,1)S(1)}, bf16[8,128,128]{2,1,0:T(8,128)(2,1)S(1)}, u32[]{:S(2)}, u32[]{:S(2)}) collective-permute-start(bf16[8,128,128]{2,1,0:T(8,128)(2,1)S(1)} %get-tuple-element.34), channel_id=1, source_target_pairs={{0,56},{8,0},{16,8},{24,16},{32,24},{40,32},{48,40},{56,48},{1,57}... | collective-permute-start | bytes 786440 | tf_op jit(solution)/shard_map/ppermute | solution.py:32
  146.0 11.1 %collective-permute-start.39 = (bf16[8,128,128]{2,1,0:T(8,128)(2,1)S(1)}, bf16[8,128,128]{2,1,0:T(8,128)(2,1)S(1)}, u32[]{:S(2)}, u32[]{:S(2)}) collective-permute-start(bf16[8,128,128]{2,1,0:T(8,128)(2,1)S(1)} %get-tuple-element.30), channel_id=1, source_target_pairs={{0,56},{8,0},{16,8},{24,16},{32,24},{40,32},{48,40},{56,48},{1,57}... | collective-permute-start | bytes 786440 | tf_op jit(solution)/shard_map/ppermute | solution.py:32
  161.1 13.8 %all-to-all-start.3 = ((bf16[16,2,2,32,128]{4,3,2,1,0:T(8,128)(2,1)}), bf16[16,2,2,32,128]{4,3,2,1,0:T(8,128)(2,1)S(1)}, u32[]{:S(2)}, u32[]{:S(2)}) async-start(bf16[16,2,2,32,128]{4,3,2,1,0:T(8,128)(2,1)} %bitcast.7), calls=%async_computation.3 | async-start | bytes 1048576 | tf_op jit(solution)/shard_map/all_to_all | solution.py:335
  (33 other events, 245.4 us)

commit v2 on v1

--- a/solution.py
+++ b/solution.py
@@ -82,8 +82,7 @@
 
     for load in loads:
         load.start()
-    for part in range(X):
-        token_load(part).start()
+    token_load(0).start()
 
     def clear(i, _):
         dk[i] = jnp.zeros((NBLEN, HS), F32)
@@ -101,6 +100,10 @@
         @pl.when(inner == 0)
         def _():
             token_load(part).wait()
+
+        @pl.when(jnp.logical_and(inner == 0, part + 1 < X))
+        def _():
+            token_load(part + 1).start()
 
         q_ref, g_ref = tbuf.at[part, 0], tbuf.at[part, 1]
         att_ref, gq_ref = obuf.at[part, 0], obuf.at[part, 1]
@@ -139,8 +142,14 @@
     lax.fori_loop(0, X * steps_per_part, body, 0)
 
     stores = []
-    spans = ((HALF + N_EARLY, SLOTS), (HALF, HALF + N_EARLY), (0, HALF))
-    for piece, (first, last) in enumerate(spans):
+    middle = HALF // 2
+    pieces = (
+        (HALF + N_EARLY, SLOTS, 0, 0),
+        (HALF, HALF + N_EARLY, 1, 0),
+        (0, middle, 2, 0),
+        (middle, HALF, 2, middle),
+    )
+    for piece, (first, last, out, at) in enumerate(pieces):
         for which, (sums, outs) in enumerate(((dk, dk_outs), (dv, dv_outs))):
 
             def finish(i, _):
@@ -148,9 +157,12 @@
                 low[which, i] = (value * SCALE if which == 0 else value).astype(BF)
                 return 0
 
-            lax.fori_loop(first, last, finish, 0, unroll=2)
+            lax.fori_loop(first, last, finish, 0, unroll=4)
+            count = last - first
             store = pltpu.make_async_copy(
-                low.at[which, pl.ds(first, last - first)], outs[piece], s_sems.at[2 * piece + which]
+                low.at[which, pl.ds(first, count)],
+                outs[out].at[pl.ds(at, count)],
+                s_sems.at[2 * piece + which],
             )
             store.start()
             stores.append(store)
@@ -186,7 +198,7 @@
                 dma((X,)),
                 dma((8,)),
                 dma((X,)),
-                dma((6,)),
+                dma((8,)),
             ],
         ),
         out_shape=[jax.ShapeDtypeStruct(tokens.shape, BF)] + sums + sums,

time: 181 us -> 180 us (level)
  no operation moved by 1% of the time
where the time goes in v2:
time: 180 us; the launch traced here: 177 us
  starting transfers between devices  71.9 us (40%)
  waiting for transfers between devices  60.5 us (34%)
  Pallas kernels  35.4 us (20%)
  local copies, waits for them, and re-layouts  5.82 us (3%)
  other arithmetic  2.49 us (1%)
    ppermute x40, waiting for transfers between devices, shift(): return lax.ppermute(a, axis, [(i, (i + by) % size) for i in range(size)])  50.7 us
    ppermute x40, starting transfers between devices, shift(): return lax.ppermute(a, axis, [(i, (i + by) % size) for i in range(size)])  49.7 us
    pallas_call x1, Pallas kernels, attention(): pl.pallas_call(attention_kernel, grid_spec=pltpu.PrefetchScalarGridSpec(n...  19.1 us
    all_to_all x1, starting transfers between devices, per_device(): lax.all_to_all(both, ('head', 'x'), split_axis=0, concat_axis=0, tiled=True)  7.58 us
    all_to_all x1, waiting for transfers between devices, per_device(): lax.all_to_all(both, ('head', 'x'), split_axis=0, concat_axis=0, tiled=True)  5.6 us
    all_to_all x1, starting transfers between devices, per_device(): reply = lax.all_to_all(reply, 'x', split_axis=0, concat_axis=0, tiled=True)  5 us
    pallas_call x1, Pallas kernels, join_heads(): pl.pallas_call(kernel, grid=(tokens // rows,), in_specs=[pl.BlockSpec((X,...  4.94 us
    pallas_call x1, Pallas kernels, split_heads(): pl.pallas_call(kernel, grid=(tokens // rows,), in_specs=[wide, wide], out...  4.91 us
  transfers between devices with their start and end apart: 44, of which 20 were waited for; matrix products, arithmetic and copies ran while one was open for 3% of the time, Pallas kernels for 7%

profile of v2, /device:TPU:1, one launch (start us, length us, event | category | flops | bytes accessed | tf_op | source)
XLA Modules:
  0.0 177.1 jit_solution(14644584445725902140)
XLA Ops:
  2.5 7.6 %all-to-all-start.1 = ((bf16[16,2,2,32,128]{4,3,2,1,0:T(8,128)(2,1)}), bf16[16,2,2,32,128]{4,3,2,1,0:T(8,128)(2,1)S(1)}, u32[]{:S(2)}, u32[]{:S(2)}) async-start(bf16[16,2,2,32,128]{4,3,2,1,0:T(8,128)(2,1)} %pack_encodings.1), calls=%async_computation.1 | async-start | bytes 1048576 | tf_op jit(solution)/shard_map/all_to_all | solution.py:307
  10.1 4.9 %split_heads.1 = bf16[4,2,2048,128]{3,2,1,0:T(8,128)(2,1)} custom-call(bf16[2048,512]{1,0:T(8,128)(2,1)} %a_ref.1, bf16[2048,512]{1,0:T(8,128)(2,1)} %b_ref.1), custom_call_target="tpu_custom_call" | custom-call | tf_op jit(solution)/shard_map/split_heads/pallas_call | solution.py:221
  15.1 5.6 %all-to-all-done.1 = bf16[16,2,2,32,128]{4,3,2,1,0:T(8,128)(2,1)S(1)} async-done(((bf16[16,2,2,32,128]{4,3,2,1,0:T(8,128)(2,1)}), bf16[16,2,2,32,128]{4,3,2,1,0:T(8,128)(2,1)S(1)}, u32[]{:S(2)}, u32[]{:S(2)}) %all-to-all-start.1) | async-done | bytes 524320 | tf_op jit(solution)/shard_map/all_to_all | solution.py:307
  20.6 4.9 %all-to-all-start = ((bf16[4,2,2048,128]{3,2,1,0:T(8,128)(2,1)}), bf16[4,2,2048,128]{3,2,1,0:T(8,128)(2,1)}, u32[]{:S(2)}, u32[]{:S(2)}) async-start(bf16[4,2,2048,128]{3,2,1,0:T(8,128)(2,1)} %split_heads.1), calls=%async_computation | async-start | bytes 8388608 | tf_op jit(solution)/shard_map/all_to_all | solution.py:312
  25.6 5.7 %collective-permute-start.1 = (bf16[8,128,128]{2,1,0:T(8,128)(2,1)S(1)}, bf16[8,128,128]{2,1,0:T(8,128)(2,1)S(1)}, u32[]{:S(2)}, u32[]{:S(2)}) collective-permute-start(bf16[8,128,128]{2,1,0:T(8,128)(2,1)S(1)} %bitcast.13), channel_id=1, source_target_pairs={{0,56},{8,0},{16,8},{24,16},{32,24},{40,32},{48,40},{56,48},{1,57}... | collective-permute-start | bytes 786440 | tf_op jit(solution)/shard_map/ppermute | solution.py:32
  34.9 3.5 %collective-permute-start.3 = (bf16[8,128,128]{2,1,0:T(8,128)(2,1)S(1)}, bf16[8,128,128]{2,1,0:T(8,128)(2,1)S(1)}, u32[]{:S(2)}, u32[]{:S(2)}) collective-permute-start(bf16[8,128,128]{2,1,0:T(8,128)(2,1)S(1)} %collective-permute-done.1), channel_id=1, source_target_pairs={{0,56},{8,0},{16,8},{24,16},{32,24},{40,32},{48,40},{56,48},{1,57}... | collective-permute-start | bytes 786440 | tf_op jit(solution)/shard_map/ppermute | solution.py:32
  40.5 3.5 %collective-permute-start.13 = (bf16[8,128,128]{2,1,0:T(8,128)(2,1)S(1)}, bf16[8,128,128]{2,1,0:T(8,128)(2,1)S(1)}, u32[]{:S(2)}, u32[]{:S(2)}) collective-permute-start(bf16[8,128,128]{2,1,0:T(8,128)(2,1)S(1)} %collective-permute-done.11), channel_id=1, source_target_pairs={{0,56},{8,0},{16,8},{24,16},{32,24},{40,32},{48,40},{56,48},{1,57}... | collective-permute-start | bytes 786440 | tf_op jit(solution)/shard_map/ppermute | solution.py:32
  46.1 3.5 %collective-permute-start.5 = (bf16[8,128,128]{2,1,0:T(8,128)(2,1)S(1)}, bf16[8,128,128]{2,1,0:T(8,128)(2,1)S(1)}, u32[]{:S(2)}, u32[]{:S(2)}) collective-permute-start(bf16[8,128,128]{2,1,0:T(8,128)(2,1)S(1)} %collective-permute-done.3), channel_id=1, source_target_pairs={{0,56},{8,0},{16,8},{24,16},{32,24},{40,32},{48,40},{56,48},{1,57}... | collective-permute-start | bytes 786440 | tf_op jit(solution)/shard_map/ppermute | solution.py:32
  51.8 3.5 %collective-permute-start.15 = (bf16[8,128,128]{2,1,0:T(8,128)(2,1)S(1)}, bf16[8,128,128]{2,1,0:T(8,128)(2,1)S(1)}, u32[]{:S(2)}, u32[]{:S(2)}) collective-permute-start(bf16[8,128,128]{2,1,0:T(8,128)(2,1)S(1)} %collective-permute-done.13), channel_id=1, source_target_pairs={{0,56},{8,0},{16,8},{24,16},{32,24},{40,32},{48,40},{56,48},{1,57}... | collective-permute-start | bytes 786440 | tf_op jit(solution)/shard_map/ppermute | solution.py:32
  55.4 5.7 %collective-permute-start.18 = (bf16[40,128,128]{2,1,0:T(8,128)(2,1)S(1)}, bf16[40,128,128]{2,1,0:T(8,128)(2,1)}, u32[]{:S(2)}, u32[]{:S(2)}) collective-permute-start(bf16[40,128,128]{2,1,0:T(8,128)(2,1)S(1)} %constant_dynamic-update-slice_fusion.9.refs_4_), channel_id=1, source_target_pairs={{0,4},{4,0},{1,5},{5,1},{2,6},{6,2},{3,7},{7,3},{8,12},{12,8},{9,1... | collective-permute-start | bytes 3932168 | tf_op jit(solution)/shard_map/ppermute | solution.py:32
  62.8 3.7 %collective-permute-start.7 = (bf16[4,128,128]{2,1,0:T(8,128)(2,1)S(1)}, bf16[4,128,128]{2,1,0:T(8,128)(2,1)S(1)}, u32[]{:S(2)}, u32[]{:S(2)}) collective-permute-start(bf16[4,128,128]{2,1,0:T(8,128)(2,1)S(1)} %slice.188), channel_id=1, source_target_pairs={{0,56},{8,0},{16,8},{24,16},{32,24},{40,32},{48,40},{56,48},{1,57}... | collective-permute-start | bytes 393224 | tf_op jit(solution)/shard_map/ppermute | solution.py:32
  66.6 3.6 %collective-permute-done.14 = bf16[8,128,128]{2,1,0:T(8,128)(2,1)S(1)} collective-permute-done((bf16[8,128,128]{2,1,0:T(8,128)(2,1)S(1)}, bf16[8,128,128]{2,1,0:T(8,128)(2,1)S(1)}, u32[]{:S(2)}, u32[]{:S(2)}) %collective-permute-start.14) | collective-permute-done | bytes 262176 | tf_op jit(solution)/shard_map/ppermute | solution.py:32
  83.6 19.1 %attention.1 = (bf16[4,2,2048,128]{3,2,1,0:T(8,128)(2,1)}, bf16[24,128,128]{2,1,0:T(8,128)(2,1)}, bf16[40,128,128]{2,1,0:T(8,128)(2,1)}, bf16[64,128,128]{2,1,0:...) custom-call(s32[128]{0:T(128)} %fusion.8.ids, ...), custom_call_target="tpu_custom_call" | custom-call | tf_op jit(solution)/shard_map/attention/pallas_call | solution.py:183
  103.3 5.0 %all-to-all-start.2 = ((bf16[4,2,2048,128]{3,2,1,0:T(8,128)(2,1)}), bf16[4,2,2048,128]{3,2,1,0:T(8,128)(2,1)}, u32[]{:S(2)}, u32[]{:S(2)}) async-start(bf16[4,2,2048,128]{3,2,1,0:T(8,128)(2,1)} %get-tuple-element.23), calls=%async_computation.2 | async-start | bytes 8388608 | tf_op jit(solution)/shard_map/all_to_all | solution.py:330
  117.1 4.8 %collective-permute-done.32 = bf16[4,128,128]{2,1,0:T(8,128)(2,1)S(1)} collective-permute-done((bf16[4,128,128]{2,1,0:T(8,128)(2,1)S(1)}, bf16[4,128,128]{2,1,0:T(8,128)(2,1)S(1)}, u32[]{:S(2)}, u32[]{:S(2)}) %collective-permute-start.32) | collective-permute-done | bytes 131104 | tf_op jit(solution)/shard_map/ppermute | solution.py:32
  123.6 3.7 %collective-permute-done.23 = bf16[8,128,128]{2,1,0:T(8,128)(2,1)S(1)} collective-permute-done((bf16[8,128,128]{2,1,0:T(8,128)(2,1)S(1)}, bf16[8,128,128]{2,1,0:T(8,128)(2,1)S(1)}, u32[]{:S(2)}, u32[]{:S(2)}) %collective-permute-start.23) | collective-permute-done | bytes 262176 | tf_op jit(solution)/shard_map/ppermute | solution.py:32
  129.2 3.8 %collective-permute-done.33 = bf16[8,128,128]{2,1,0:T(8,128)(2,1)S(1)} collective-permute-done((bf16[8,128,128]{2,1,0:T(8,128)(2,1)S(1)}, bf16[8,128,128]{2,1,0:T(8,128)(2,1)S(1)}, u32[]{:S(2)}, u32[]{:S(2)}) %collective-permute-start.33) | collective-permute-done | bytes 262176 | tf_op jit(solution)/shard_map/ppermute | solution.py:32
  135.7 3.9 %collective-permute-done.28 = bf16[8,128,128]{2,1,0:T(8,128)(2,1)S(1)} collective-permute-done((bf16[8,128,128]{2,1,0:T(8,128)(2,1)S(1)}, bf16[8,128,128]{2,1,0:T(8,128)(2,1)S(1)}, u32[]{:S(2)}, u32[]{:S(2)}) %collective-permute-start.28) | collective-permute-done | bytes 262176 | tf_op jit(solution)/shard_map/ppermute | solution.py:32
  141.3 4.0 %collective-permute-done.38 = bf16[8,128,128]{2,1,0:T(8,128)(2,1)S(1)} collective-permute-done((bf16[8,128,128]{2,1,0:T(8,128)(2,1)S(1)}, bf16[8,128,128]{2,1,0:T(8,128)(2,1)S(1)}, u32[]{:S(2)}, u32[]{:S(2)}) %collective-permute-start.38) | collective-permute-done | bytes 262176 | tf_op jit(solution)/shard_map/ppermute | solution.py:32
  146.9 4.0 %collective-permute-done.29.refs_3_ = bf16[8,128,128]{2,1,0:T(8,128)(2,1)S(1)} collective-permute-done((bf16[8,128,128]{2,1,0:T(8,128)(2,1)S(1)}, bf16[8,128,128]{2,1,0:T(8,128)(2,1)S(1)}, u32[]{:S(2)}, u32[]{:S(2)}) %collective-permute-start.29) | collective-permute-done | bytes 262176 | tf_op jit(solution)/shard_map/ppermute | solution.py:32
  150.9 5.6 %collective-permute-done.39.refs_7_ = bf16[8,128,128]{2,1,0:T(8,128)(2,1)S(1)} collective-permute-done((bf16[8,128,128]{2,1,0:T(8,128)(2,1)S(1)}, bf16[8,128,128]{2,1,0:T(8,128)(2,1)S(1)}, u32[]{:S(2)}, u32[]{:S(2)}) %collective-permute-start.39) | collective-permute-done | bytes 262176 | tf_op jit(solution)/shard_map/ppermute | solution.py:32
  160.5 4.7 %all-to-all-start.3 = ((bf16[16,2,2,32,128]{4,3,2,1,0:T(8,128)(2,1)}), bf16[16,2,2,32,128]{4,3,2,1,0:T(8,128)(2,1)S(1)}, u32[]{:S(2)}, u32[]{:S(2)}) async-start(bf16[16,2,2,32,128]{4,3,2,1,0:T(8,128)(2,1)} %bitcast.7), calls=%async_computation.3 | async-start | bytes 1048576 | tf_op jit(solution)/shard_map/all_to_all | solution.py:347
  165.2 4.9 %join_heads.1 = (bf16[2048,512]{1,0:T(8,128)(2,1)}, bf16[2048,512]{1,0:T(8,128)(2,1)}) custom-call(bf16[4,2,2048,128]{3,2,1,0:T(8,128)(2,1)} %all-to-all-done.2.a_ref), custom_call_target="tpu_custom_call" | custom-call | tf_op jit(solution)/shard_map/join_heads/pallas_call | solution.py:242
  170.2 4.2 %all-to-all-done.3.a_ref = bf16[16,2,2,32,128]{4,3,2,1,0:T(8,128)(2,1)S(1)} async-done(((bf16[16,2,2,32,128]{4,3,2,1,0:T(8,128)(2,1)}), bf16[16,2,2,32,128]{4,3,2,1,0:T(8,128)(2,1)S(1)}, u32[]{:S(2)}, u32[]{:S(2)}) %all-to-all-start.3) | async-done | bytes 524320 | tf_op jit(solution)/shard_map/all_to_all | solution.py:347
  (140 shorter events, 52.8 us)
Async XLA Ops:
  2.5 18.1 %all-to-all-start.1 = ((bf16[16,2,2,32,128]{4,3,2,1,0:T(8,128)(2,1)}), bf16[16,2,2,32,128]{4,3,2,1,0:T(8,128)(2,1)S(1)}, u32[]{:S(2)}, u32[]{:S(2)}) async-start(bf16[16,2,2,32,128]{4,3,2,1,0:T(8,128)(2,1)} %pack_encodings.1), calls=%async_computation.1 | async-start | bytes 1048576 | tf_op jit(solution)/shard_map/all_to_all | solution.py:307
  20.6 63.0 %all-to-all-start = ((bf16[4,2,2048,128]{3,2,1,0:T(8,128)(2,1)}), bf16[4,2,2048,128]{3,2,1,0:T(8,128)(2,1)}, u32[]{:S(2)}, u32[]{:S(2)}) async-start(bf16[4,2,2048,128]{3,2,1,0:T(8,128)(2,1)} %split_heads.1), calls=%async_computation | async-start | bytes 8388608 | tf_op jit(solution)/shard_map/all_to_all | solution.py:312
  34.9 11.2 %collective-permute-start.3 = (bf16[8,128,128]{2,1,0:T(8,128)(2,1)S(1)}, bf16[8,128,128]{2,1,0:T(8,128)(2,1)S(1)}, u32[]{:S(2)}, u32[]{:S(2)}) collective-permute-start(bf16[8,128,128]{2,1,0:T(8,128)(2,1)S(1)} %collective-permute-done.1), channel_id=1, source_target_pairs={{0,56},{8,0},{16,8},{24,16},{32,24},{40,32},{48,40},{56,48},{1,57}... | collective-permute-start | bytes 786440 | tf_op jit(solution)/shard_map/ppermute | solution.py:32
  38.4 11.2 %collective-permute-start.2 = (bf16[8,128,128]{2,1,0:T(8,128)(2,1)S(1)}, bf16[8,128,128]{2,1,0:T(8,128)(2,1)S(1)}, u32[]{:S(2)}, u32[]{:S(2)}) collective-permute-start(bf16[8,128,128]{2,1,0:T(8,128)(2,1)S(1)} %collective-permute-done), channel_id=1, source_target_pairs={{0,8},{8,16},{16,24},{24,32},{32,40},{40,48},{48,56},{56,0},{1,9},... | collective-permute-start | bytes 786440 | tf_op jit(solution)/shard_map/ppermute | solution.py:32
  40.5 11.2 %collective-permute-start.13 = (bf16[8,128,128]{2,1,0:T(8,128)(2,1)S(1)}, bf16[8,128,128]{2,1,0:T(8,128)(2,1)S(1)}, u32[]{:S(2)}, u32[]{:S(2)}) collective-permute-start(bf16[8,128,128]{2,1,0:T(8,128)(2,1)S(1)} %collective-permute-done.11), channel_id=1, source_target_pairs={{0,56},{8,0},{16,8},{24,16},{32,24},{40,32},{48,40},{56,48},{1,57}... | collective-permute-start | bytes 786440 | tf_op jit(solution)/shard_map/ppermute | solution.py:32
  44.0 11.2 %collective-permute-start.12 = (bf16[8,128,128]{2,1,0:T(8,128)(2,1)S(1)}, bf16[8,128,128]{2,1,0:T(8,128)(2,1)S(1)}, u32[]{:S(2)}, u32[]{:S(2)}) collective-permute-start(bf16[8,128,128]{2,1,0:T(8,128)(2,1)S(1)} %collective-permute-done.10), channel_id=1, source_target_pairs={{0,8},{8,16},{16,24},{24,32},{32,40},{40,48},{48,56},{56,0},{1,9},... | collective-permute-start | bytes 786440 | tf_op jit(solution)/shard_map/ppermute | solution.py:32
  46.1 15.0 %collective-permute-start.5 = (bf16[8,128,128]{2,1,0:T(8,128)(2,1)S(1)}, bf16[8,128,128]{2,1,0:T(8,128)(2,1)S(1)}, u32[]{:S(2)}, u32[]{:S(2)}) collective-permute-start(bf16[8,128,128]{2,1,0:T(8,128)(2,1)S(1)} %collective-permute-done.3), channel_id=1, source_target_pairs={{0,56},{8,0},{16,8},{24,16},{32,24},{40,32},{48,40},{56,48},{1,57}... | collective-permute-start | bytes 786440 | tf_op jit(solution)/shard_map/ppermute | solution.py:32
  49.7 13.1 %collective-permute-start.4 = (bf16[8,128,128]{2,1,0:T(8,128)(2,1)S(1)}, bf16[8,128,128]{2,1,0:T(8,128)(2,1)S(1)}, u32[]{:S(2)}, u32[]{:S(2)}) collective-permute-start(bf16[8,128,128]{2,1,0:T(8,128)(2,1)S(1)} %collective-permute-done.2), channel_id=1, source_target_pairs={{0,8},{8,16},{16,24},{24,32},{32,40},{40,48},{48,56},{56,0},{1,9},... | collective-permute-start | bytes 786440 | tf_op jit(solution)/shard_map/ppermute | solution.py:32
  51.8 14.7 %collective-permute-start.15 = (bf16[8,128,128]{2,1,0:T(8,128)(2,1)S(1)}, bf16[8,128,128]{2,1,0:T(8,128)(2,1)S(1)}, u32[]{:S(2)}, u32[]{:S(2)}) collective-permute-start(bf16[8,128,128]{2,1,0:T(8,128)(2,1)S(1)} %collective-permute-done.13), channel_id=1, source_target_pairs={{0,56},{8,0},{16,8},{24,16},{32,24},{40,32},{48,40},{56,48},{1,57}... | collective-permute-start | bytes 786440 | tf_op jit(solution)/shard_map/ppermute | solution.py:32
  55.4 28.2 %collective-permute-start.18 = (bf16[40,128,128]{2,1,0:T(8,128)(2,1)S(1)}, bf16[40,128,128]{2,1,0:T(8,128)(2,1)}, u32[]{:S(2)}, u32[]{:S(2)}) collective-permute-start(bf16[40,128,128]{2,1,0:T(8,128)(2,1)S(1)} %constant_dynamic-update-slice_fusion.9.refs_4_), channel_id=1, source_target_pairs={{0,4},{4,0},{1,5},{5,1},{2,6},{6,2},{3,7},{7,3},{8,12},{12,8},{9,1... | collective-permute-start | bytes 3932168 | tf_op jit(solution)/shard_map/ppermute | solution.py:32
  61.1 22.5 %collective-permute-start.8 = (bf16[40,128,128]{2,1,0:T(8,128)(2,1)S(1)}, bf16[40,128,128]{2,1,0:T(8,128)(2,1)}, u32[]{:S(2)}, u32[]{:S(2)}) collective-permute-start(bf16[40,128,128]{2,1,0:T(8,128)(2,1)S(1)} %constant_dynamic-update-slice_fusion.refs_0_), channel_id=1, source_target_pairs={{0,4},{4,0},{1,5},{5,1},{2,6},{6,2},{3,7},{7,3},{8,12},{12,8},{9,1... | collective-permute-start | bytes 3932168 | tf_op jit(solution)/shard_map/ppermute | solution.py:32
  62.8 10.5 %collective-permute-start.7 = (bf16[4,128,128]{2,1,0:T(8,128)(2,1)S(1)}, bf16[4,128,128]{2,1,0:T(8,128)(2,1)S(1)}, u32[]{:S(2)}, u32[]{:S(2)}) collective-permute-start(bf16[4,128,128]{2,1,0:T(8,128)(2,1)S(1)} %slice.188), channel_id=1, source_target_pairs={{0,56},{8,0},{16,8},{24,16},{32,24},{40,32},{48,40},{56,48},{1,57}... | collective-permute-start | bytes 393224 | tf_op jit(solution)/shard_map/ppermute | solution.py:32
  103.3 57.2 %all-to-all-start.2 = ((bf16[4,2,2048,128]{3,2,1,0:T(8,128)(2,1)}), bf16[4,2,2048,128]{3,2,1,0:T(8,128)(2,1)}, u32[]{:S(2)}, u32[]{:S(2)}) async-start(bf16[4,2,2048,128]{3,2,1,0:T(8,128)(2,1)} %get-tuple-element.23), calls=%async_computation.2 | async-start | bytes 8388608 | tf_op jit(solution)/shard_map/all_to_all | solution.py:330
  108.3 19.2 %collective-permute-start.20 = (bf16[40,128,128]{2,1,0:T(8,128)(2,1)}, bf16[40,128,128]{2,1,0:T(8,128)(2,1)S(1)}, u32[]{:S(2)}, u32[]{:S(2)}) collective-permute-start(bf16[40,128,128]{2,1,0:T(8,128)(2,1)} %get-tuple-element.18), channel_id=1, source_target_pairs={{0,4},{4,0},{1,5},{5,1},{2,6},{6,2},{3,7},{7,3},{8,12},{12,8},{9,1... | collective-permute-start | bytes 3932168 | tf_op jit(solution)/shard_map/ppermute | solution.py:32
  108.8 25.3 %collective-permute-start.30 = (bf16[40,128,128]{2,1,0:T(8,128)(2,1)}, bf16[40,128,128]{2,1,0:T(8,128)(2,1)S(1)}, u32[]{:S(2)}, u32[]{:S(2)}) collective-permute-start(bf16[40,128,128]{2,1,0:T(8,128)(2,1)} %get-tuple-element.21), channel_id=1, source_target_pairs={{0,4},{4,0},{1,5},{5,1},{2,6},{6,2},{3,7},{7,3},{8,12},{12,8},{9,1... | collective-permute-start | bytes 3932168 | tf_op jit(solution)/shard_map/ppermute | solution.py:32
  116.5 10.8 %collective-permute-start.23 = (bf16[8,128,128]{2,1,0:T(8,128)(2,1)S(1)}, bf16[8,128,128]{2,1,0:T(8,128)(2,1)S(1)}, u32[]{:S(2)}, u32[]{:S(2)}) collective-permute-start(bf16[8,128,128]{2,1,0:T(8,128)(2,1)S(1)} %pad_maximum_fusion), channel_id=1, source_target_pairs={{0,8},{8,16},{16,24},{24,32},{32,40},{40,48},{48,56},{56,0},{1,9},... | collective-permute-start | bytes 786440 | tf_op jit(solution)/shard_map/ppermute | solution.py:32
  122.0 10.9 %collective-permute-start.33 = (bf16[8,128,128]{2,1,0:T(8,128)(2,1)S(1)}, bf16[8,128,128]{2,1,0:T(8,128)(2,1)S(1)}, u32[]{:S(2)}, u32[]{:S(2)}) collective-permute-start(bf16[8,128,128]{2,1,0:T(8,128)(2,1)S(1)} %pad_maximum_fusion.2), channel_id=1, source_target_pairs={{0,8},{8,16},{16,24},{24,32},{32,40},{40,48},{48,56},{56,0},{1,9},... | collective-permute-start | bytes 786440 | tf_op jit(solution)/shard_map/ppermute | solution.py:32
  127.6 12.0 %collective-permute-start.28 = (bf16[8,128,128]{2,1,0:T(8,128)(2,1)S(1)}, bf16[8,128,128]{2,1,0:T(8,128)(2,1)S(1)}, u32[]{:S(2)}, u32[]{:S(2)}) collective-permute-start(bf16[8,128,128]{2,1,0:T(8,128)(2,1)S(1)} %get-tuple-element.36), channel_id=1, source_target_pairs={{0,56},{8,0},{16,8},{24,16},{32,24},{40,32},{48,40},{56,48},{1,57}... | collective-permute-start | bytes 786440 | tf_op jit(solution)/shard_map/ppermute | solution.py:32
  128.9 10.8 %collective-permute-start.24 = (bf16[8,128,128]{2,1,0:T(8,128)(2,1)S(1)}, bf16[8,128,128]{2,1,0:T(8,128)(2,1)S(1)}, u32[]{:S(2)}, u32[]{:S(2)}) collective-permute-start(bf16[8,128,128]{2,1,0:T(8,128)(2,1)S(1)} %get-tuple-element.37), channel_id=1, source_target_pairs={{0,8},{8,16},{16,24},{24,32},{32,40},{40,48},{48,56},{56,0},{1,9},... | collective-permute-start | bytes 786440 | tf_op jit(solution)/shard_map/ppermute | solution.py:32
  134.2 11.1 %collective-permute-start.38 = (bf16[8,128,128]{2,1,0:T(8,128)(2,1)S(1)}, bf16[8,128,128]{2,1,0:T(8,128)(2,1)S(1)}, u32[]{:S(2)}, u32[]{:S(2)}) collective-permute-start(bf16[8,128,128]{2,1,0:T(8,128)(2,1)S(1)} %get-tuple-element.32), channel_id=1, source_target_pairs={{0,56},{8,0},{16,8},{24,16},{32,24},{40,32},{48,40},{56,48},{1,57}... | collective-permute-start | bytes 786440 | tf_op jit(solution)/shard_map/ppermute | solution.py:32
  135.0 10.3 %collective-permute-start.34 = (bf16[8,128,128]{2,1,0:T(8,128)(2,1)S(1)}, bf16[8,128,128]{2,1,0:T(8,128)(2,1)S(1)}, u32[]{:S(2)}, u32[]{:S(2)}) collective-permute-start(bf16[8,128,128]{2,1,0:T(8,128)(2,1)S(1)} %get-tuple-element.33), channel_id=1, source_target_pairs={{0,8},{8,16},{16,24},{24,32},{32,40},{40,48},{48,56},{56,0},{1,9},... | collective-permute-start | bytes 786440 | tf_op jit(solution)/shard_map/ppermute | solution.py:32
  139.7 11.1 %collective-permute-start.29 = (bf16[8,128,128]{2,1,0:T(8,128)(2,1)S(1)}, bf16[8,128,128]{2,1,0:T(8,128)(2,1)S(1)}, u32[]{:S(2)}, u32[]{:S(2)}) collective-permute-start(bf16[8,128,128]{2,1,0:T(8,128)(2,1)S(1)} %get-tuple-element.34), channel_id=1, source_target_pairs={{0,56},{8,0},{16,8},{24,16},{32,24},{40,32},{48,40},{56,48},{1,57}... | collective-permute-start | bytes 786440 | tf_op jit(solution)/shard_map/ppermute | solution.py:32
  145.4 11.1 %collective-permute-start.39 = (bf16[8,128,128]{2,1,0:T(8,128)(2,1)S(1)}, bf16[8,128,128]{2,1,0:T(8,128)(2,1)S(1)}, u32[]{:S(2)}, u32[]{:S(2)}) collective-permute-start(bf16[8,128,128]{2,1,0:T(8,128)(2,1)S(1)} %get-tuple-element.30), channel_id=1, source_target_pairs={{0,56},{8,0},{16,8},{24,16},{32,24},{40,32},{48,40},{56,48},{1,57}... | collective-permute-start | bytes 786440 | tf_op jit(solution)/shard_map/ppermute | solution.py:32
  160.5 13.8 %all-to-all-start.3 = ((bf16[16,2,2,32,128]{4,3,2,1,0:T(8,128)(2,1)}), bf16[16,2,2,32,128]{4,3,2,1,0:T(8,128)(2,1)S(1)}, u32[]{:S(2)}, u32[]{:S(2)}) async-start(bf16[16,2,2,32,128]{4,3,2,1,0:T(8,128)(2,1)} %bitcast.7), calls=%async_computation.3 | async-start | bytes 1048576 | tf_op jit(solution)/shard_map/all_to_all | solution.py:347
  (33 other events, 245.4 us)
